TPU v7x, 32 devices: a whole 2x2x4 slice. The times are simulated.
32 devices in a mesh: dp: 8 (over y, x, core), seq: 4 (over z).
Axes of the slice: x: 2, y: 2, z: 4, core: 2. Of those that a mesh axis runs over, the one named last changes fastest.
Arguments:
- inputs: bfloat16 [8, 3072, 768], P('dp', 'seq'), may hold values from -6 to 6
- pass_embed: bfloat16 [768], P('dp'), may hold values from -3 to 3
- gain_attend: bfloat16 [768], P('dp'), may hold values from 0.25 to 1.75
- shift_attend: bfloat16 [768], P('dp'), may hold values from -3 to 3
- attend_in: bfloat16 [768, 2304], P('dp'), may hold values from -0.21875 to 0.21875
- attend_out: bfloat16 [768, 768], P('dp'), may hold values from -0.875 to 0.875
- gain_hidden: bfloat16 [768], P('dp'), may hold values from 0.25 to 1.75
- shift_hidden: bfloat16 [768], P('dp'), may hold values from -3 to 3
- hidden_up: bfloat16 [768, 3072], P('dp'), may hold values from -0.21875 to 0.21875
- hidden_down: bfloat16 [3072, 768], P('dp'), may hold values from -0.109375 to 0.109375
- cotangent: bfloat16 [8, 3072, 768], P('dp', 'seq'), may hold values from -6 to 6
Outputs:
- layer_out: bfloat16 [8, 3072, 768], P('dp', 'seq')
- input_grad: float32 [8, 3072, 768], P('dp', 'seq')
- embed_grad: float32 [768], P('dp')
- gain_attend_grad: float32 [768], P('dp')
- shift_attend_grad: float32 [768], P('dp')
- attend_in_grad: float32 [768, 2304], P('dp')
- attend_out_grad: float32 [768, 768], P('dp')
- gain_hidden_grad: float32 [768], P('dp')
- shift_hidden_grad: float32 [768], P('dp')
- hidden_up_grad: float32 [768, 3072], P('dp')
- hidden_down_grad: float32 [3072, 768], P('dp')
All inputs are finite; a program needn't handle non-finite values.
Results may differ from a plain program's by a relative error of at most 0.007.
Values may be sent and summed in bfloat16 or wider, within the bound.
No kernel may reach another device: no remote copies, remote signals or barrier semaphores. Data moves between devices by JAX's collectives and lax.ppermute only.
A program may use at most 192 MiB of HBM per device.

v0:
```python
import jax
import jax.numpy as jnp
from jax import lax
from jax.sharding import PartitionSpec as P

HD = 64


EPSILON = 1e-05
MASKED = -1e30


def layer_norm(hidden, gain, shift):
    center = hidden - jnp.mean(hidden, axis=-1, keepdims=True)
    spread = jnp.mean(center * center, axis=-1, keepdims=True)
    return center * lax.rsqrt(spread + EPSILON) * gain + shift


def gelu_tanh(pre_act):
    return jax.nn.gelu(pre_act, approximate=True)


def causal_scores(query_blk, keys, first_row, score_scale):
    block_rows = query_blk.shape[0]
    scores = (
        jnp.einsum("qhd,khd->hqk", query_blk, keys, preferred_element_type=jnp.float32)
        * score_scale
    )
    query_pos = first_row + jnp.arange(block_rows, dtype=jnp.int32)
    key_pos = jnp.arange(keys.shape[0], dtype=jnp.int32)
    causal = key_pos[None, :] <= query_pos[:, None]
    return jnp.where(causal[None], scores, MASKED)


def attend_forward(queries, keys, values):
    length, heads_dev, head_dim = queries.shape
    block_rows = min(512, length)
    score_scale = head_dim ** (-0.5)

    def attend_one(block_idx):
        first_row = block_idx * block_rows
        query_blk = lax.dynamic_slice_in_dim(queries, first_row, block_rows, 0)
        scores = causal_scores(query_blk, keys, first_row, score_scale)
        row_max = jnp.max(scores, axis=-1, keepdims=True)
        raw_weights = jnp.exp(scores - row_max)
        row_sum = jnp.sum(raw_weights, axis=-1, keepdims=True)
        probs = (raw_weights / row_sum).astype(jnp.bfloat16)
        result = jnp.einsum("hqk,khd->qhd", probs, values, preferred_element_type=jnp.float32)
        return (result.astype(jnp.bfloat16), (row_max + jnp.log(row_sum))[..., 0])

    blocks, logsum = lax.map(attend_one, jnp.arange(length // block_rows, dtype=jnp.int32))
    return (blocks.reshape(length, heads_dev * head_dim), logsum)


def attend_backward(queries, keys, values, grad_out, logsum):
    length, heads_dev, head_dim = queries.shape
    block_rows = min(512, length)
    score_scale = head_dim ** (-0.5)

    def attend_back(running, block_idx):
        grad_keys, grad_values = running
        first_row = block_idx * block_rows
        query_blk = lax.dynamic_slice_in_dim(queries, first_row, block_rows, 0)
        grad_blk = lax.dynamic_slice_in_dim(grad_out, first_row, block_rows, 0)
        scores = causal_scores(query_blk, keys, first_row, score_scale)
        probs = jnp.exp(scores - logsum[block_idx][:, :, None])
        probs_low = probs.astype(jnp.bfloat16)
        grad_values = grad_values + jnp.einsum(
            "hqk,qhd->khd", probs_low, grad_blk, preferred_element_type=jnp.float32
        )
        grad_probs = jnp.einsum(
            "qhd,khd->hqk", grad_blk, values, preferred_element_type=jnp.float32
        )
        grad_scores = (
            probs * (grad_probs - jnp.sum(probs * grad_probs, axis=-1, keepdims=True))
        ).astype(jnp.bfloat16)
        grad_query = (
            jnp.einsum("hqk,khd->qhd", grad_scores, keys, preferred_element_type=jnp.float32)
            * score_scale
        )
        grad_keys = (
            grad_keys
            + jnp.einsum("hqk,qhd->khd", grad_scores, query_blk, preferred_element_type=jnp.float32)
            * score_scale
        )
        return ((grad_keys, grad_values), grad_query.astype(jnp.bfloat16))

    zeros_init = jnp.zeros((length, heads_dev, head_dim), jnp.float32)
    (grad_keys, grad_values), grad_blocks = lax.scan(
        attend_back, (zeros_init, zeros_init), jnp.arange(length // block_rows, dtype=jnp.int32)
    )
    flat_width = heads_dev * head_dim
    return (
        grad_blocks.reshape(length, flat_width),
        grad_keys.astype(jnp.bfloat16).reshape(length, flat_width),
        grad_values.astype(jnp.bfloat16).reshape(length, flat_width),
    )


def on_device(
    inputs,
    pass_embed,
    gain_attend,
    shift_attend,
    attend_in,
    attend_out,
    gain_hidden,
    shift_hidden,
    hidden_up,
    hidden_down,
    cotangent,
):
    gathered = (
        lax.all_gather(pass_embed, "dp", axis=0, tiled=True),
        lax.all_gather(gain_attend, "dp", axis=0, tiled=True),
        lax.all_gather(shift_attend, "dp", axis=0, tiled=True),
        lax.all_gather(attend_in, "dp", axis=0, tiled=True),
        lax.all_gather(attend_out, "dp", axis=0, tiled=True),
        lax.all_gather(gain_hidden, "dp", axis=0, tiled=True),
        lax.all_gather(shift_hidden, "dp", axis=0, tiled=True),
        lax.all_gather(hidden_up, "dp", axis=0, tiled=True),
        lax.all_gather(hidden_down, "dp", axis=0, tiled=True),
    )
    (
        embed_full,
        gain_one,
        shift_one,
        proj_in,
        proj_out,
        gain_two,
        shift_two,
        weight_up,
        weight_down,
    ) = gathered
    model_width = proj_in.shape[0]
    local_rows = inputs[0].astype(jnp.float32)
    row_count = local_rows.shape[0]
    resid_zero = local_rows + embed_full.astype(jnp.float32)
    normed_one, norm_back_one = jax.vjp(
        layer_norm, resid_zero, gain_one.astype(jnp.float32), shift_one.astype(jnp.float32)
    )
    normed_low = normed_one.astype(jnp.bfloat16)
    packed = jnp.dot(normed_low, proj_in, preferred_element_type=jnp.float32).astype(jnp.bfloat16)
    by_heads = lax.all_to_all(
        packed.reshape(row_count, 3, model_width), "seq", split_axis=2, concat_axis=0, tiled=True
    )
    length = by_heads.shape[0]
    heads_dev = by_heads.shape[2] // HD
    queries = by_heads[:, 0].reshape(length, heads_dev, HD)
    keys = by_heads[:, 1].reshape(length, heads_dev, HD)
    values = by_heads[:, 2].reshape(length, heads_dev, HD)
    attended, logsum = attend_forward(queries, keys, values)
    merged = lax.all_to_all(attended, "seq", split_axis=0, concat_axis=1, tiled=True)
    branch = jnp.dot(merged, proj_out, preferred_element_type=jnp.float32)
    resid_one = resid_zero + branch
    normed_two, norm_back_two = jax.vjp(
        layer_norm, resid_one, gain_two.astype(jnp.float32), shift_two.astype(jnp.float32)
    )
    normed_two_low = normed_two.astype(jnp.bfloat16)
    pre_act = jnp.dot(normed_two_low, weight_up, preferred_element_type=jnp.float32)
    activated, gelu_back = jax.vjp(gelu_tanh, pre_act)
    act_low = activated.astype(jnp.bfloat16)
    result = resid_one + jnp.dot(act_low, weight_down, preferred_element_type=jnp.float32)
    proj_in, proj_out, weight_up, weight_down = (
        lax.all_gather(attend_in, "dp", axis=0, tiled=True),
        lax.all_gather(attend_out, "dp", axis=0, tiled=True),
        lax.all_gather(hidden_up, "dp", axis=0, tiled=True),
        lax.all_gather(hidden_down, "dp", axis=0, tiled=True),
    )
    grad_result = cotangent[0]
    grad_down = jnp.dot(act_low.T, grad_result, preferred_element_type=jnp.float32)
    grad_act = jnp.dot(grad_result, weight_down.T, preferred_element_type=jnp.float32)
    grad_pre = gelu_back(grad_act)[0].astype(jnp.bfloat16)
    grad_up = jnp.dot(normed_two_low.T, grad_pre, preferred_element_type=jnp.float32)
    grad_normed_two = jnp.dot(grad_pre, weight_up.T, preferred_element_type=jnp.float32)
    grad_resid_two, grad_gain_two, grad_shift_two = norm_back_two(grad_normed_two)
    grad_resid_one = grad_result.astype(jnp.float32) + grad_resid_two
    grad_branch = grad_resid_one.astype(jnp.bfloat16)
    grad_proj_out = jnp.dot(merged.T, grad_branch, preferred_element_type=jnp.float32)
    grad_merged = jnp.dot(grad_branch, proj_out.T, preferred_element_type=jnp.float32).astype(
        jnp.bfloat16
    )
    grad_heads = lax.all_to_all(grad_merged, "seq", split_axis=1, concat_axis=0, tiled=True)
    grad_query, grad_keys, grad_values = attend_backward(
        queries, keys, values, grad_heads.reshape(length, heads_dev, HD), logsum
    )
    grad_packed = jnp.stack([grad_query, grad_keys, grad_values], axis=1)
    grad_spans = lax.all_to_all(
        grad_packed, "seq", split_axis=0, concat_axis=2, tiled=True
    ).reshape(row_count, 3 * model_width)
    grad_proj_in = jnp.dot(normed_low.T, grad_spans, preferred_element_type=jnp.float32)
    grad_normed_one = jnp.dot(grad_spans, proj_in.T, preferred_element_type=jnp.float32)
    grad_resid_norm, grad_gain_one, grad_shift_one = norm_back_one(grad_normed_one)
    grad_input = grad_resid_one + grad_resid_norm
    grad_embed = jnp.sum(grad_input, axis=0)
    shares = (
        lax.psum_scatter(grad_embed, "dp", scatter_dimension=0, tiled=True),
        lax.psum_scatter(grad_gain_one, "dp", scatter_dimension=0, tiled=True),
        lax.psum_scatter(grad_shift_one, "dp", scatter_dimension=0, tiled=True),
        lax.psum_scatter(grad_proj_in, "dp", scatter_dimension=0, tiled=True),
        lax.psum_scatter(grad_proj_out, "dp", scatter_dimension=0, tiled=True),
        lax.psum_scatter(grad_gain_two, "dp", scatter_dimension=0, tiled=True),
        lax.psum_scatter(grad_shift_two, "dp", scatter_dimension=0, tiled=True),
        lax.psum_scatter(grad_up, "dp", scatter_dimension=0, tiled=True),
        lax.psum_scatter(grad_down, "dp", scatter_dimension=0, tiled=True),
    )
    totals = lax.psum(
        (
            shares[0],
            shares[1],
            shares[2],
            shares[3],
            shares[4],
            shares[5],
            shares[6],
            shares[7],
            shares[8],
        ),
        "seq",
    )
    return (
        result.astype(jnp.bfloat16)[None],
        grad_input[None],
        totals[0],
        totals[1],
        totals[2],
        totals[3],
        totals[4],
        totals[5],
        totals[6],
        totals[7],
        totals[8],
    )


def solution(mesh):
    placed = (
        P("dp", "seq", None),
        P("dp"),
        P("dp"),
        P("dp"),
        P("dp", None),
        P("dp", None),
        P("dp"),
        P("dp"),
        P("dp", None),
        P("dp", None),
        P("dp", "seq", None),
    )
    return jax.shard_map(
        on_device,
        mesh=mesh,
        in_specs=placed,
        out_specs=(
            P("dp", "seq", None),
            P("dp", "seq", None),
            P("dp"),
            P("dp"),
            P("dp"),
            P("dp", None),
            P("dp", None),
            P("dp"),
            P("dp"),
            P("dp", None),
            P("dp", None),
        ),
        check_vma=False,
    )
```

profile of v0, /device:TPU:0, one launch (start us, length us, event | category | flops | bytes accessed | tf_op | source)
XLA Modules:
  0.0 1205.8 jit_solution(13468047402046716221)
XLA Ops:
  15.6 26.0 %all-reduce.13 = (bf16[768]{0:T(1024)(128)(2,1)S(1)}, bf16[768]{0:T(1024)(128)(2,1)S(1)}, bf16[768]{0:T(1024)(128)(2,1)S(1)}, bf16[768]{0:T(1024)(128)(2,1)}, bf16[768]{0:T(1024)(128)(2,1)}) all-reduce(bf16[768]{0:T(1024)(128)(2,1)S(1)} %dynamic-update-slice.2, ...), channel_id=1, replica_groups=mesh['dp'=8,'seq'=4] {'dp'}, use_global_device_ids=true, to_apply=%add.2 | all-reduce | flops 3840 | bytes 15360
  46.8 6.8 convolution_convert_fusion
  59.4 7.2 copy.84
  72.1 104.6 %all-to-all-done = bf16[768,3,768]{0,1,2:T(4,128)(2,1)} async-done(((bf16[768,3,768]{0,1,2:T(4,128)(2,1)}), bf16[768,3,768]{0,1,2:T(4,128)(2,1)}, u32[]{:S(2)}, u32[]{:S(2)}) %all-to-all-start) | async-done | bytes 3538976 | tf_op jit(solution)/shard_map/all_to_all | solution.py:144
  183.0 129.0 %while.27 = (s32[]{:T(128)}, bf16[6,512,3,64]{1,3,2,0:T(8,128)(2,1)}, f32[6,3,512]{2,1,0:T(4,128)}, s32[6]{0:T(128)S(1)}, bf16[3072,3,64]{0,2,1:T(8,128)(2,1)}, ...) while((s32[]{:T(128)}, ...), condition=%wide.region_5.6_spmd, body=%wide.region_2.5_spmd.sunk | while | flops 1266252800 | bytes 65722560 | solution.py:51
  196.1 7.8 fusion.146
  217.6 7.8 fusion.146
  239.1 7.8 fusion.146
  260.6 7.8 fusion.146
  282.1 7.8 fusion.146
  303.6 7.8 fusion.146
  321.8 26.5 %all-to-all-done.1 = bf16[4,768,192]{1,2,0:T(8,128)(2,1)S(1)} async-done(((bf16[4,768,192]{1,2,0:T(8,128)(2,1)}), bf16[4,768,192]{1,2,0:T(8,128)(2,1)S(1)}, u32[]{:S(2)}, u32[]{:S(2)}) %all-to-all-start.1) | async-done | bytes 1179680 | tf_op jit(solution)/shard_map/all_to_all | solution.py:153
  353.2 9.1 fusion.92
  362.3 11.4 fusion.44
  391.7 12.8 %fusion.71 = f32[3072,768]{1,0:T(8,128)} fusion(bf16[1,768,768]{2,1,0:T(8,128)(2,1)S(1)} %copy-done.16, f32[768,3072]{1,0:T(8,128)} %fusion.92), kind=kOutput, calls=%fused_computation.95 | convolution fusion | flops 3645112320 | bytes 20054016 | tf_op jit(solution)/shard_map/dot_general | solution.py:171
  412.8 8.9 fusion.91
  421.7 18.8 %all-to-all-done.2 = bf16[768,4,192]{0,2,1:T(8,128)(2,1)S(1)} async-done(((bf16[768,4,192]{0,2,1:T(8,128)(2,1)}), bf16[768,4,192]{0,2,1:T(8,128)(2,1)S(1)}, u32[]{:S(2)}, u32[]{:S(2)}) %all-to-all-start.2) | async-done | bytes 1179680 | tf_op jit(solution)/shard_map/all_to_all | solution.py:183
  447.1 369.0 %while.28 = (s32[]{:T(128)}, f32[3072,3,64]{0,2,1:T(8,128)}, f32[3072,3,64]{0,2,1:T(8,128)}, bf16[6,512,3,64]{1,3,2,0:T(8,128)(2,1)}, s32[6]{0:T(128)S(1)}, /*in...) while((s32[]{:T(128)}, f32[3072,3,64]{0,2,1:T(8,128)}, ...), condition=%wide.region_12.13_spmd.clone, body=%wide.region_10.12_spmd.clone.sunk | while | flops 3095395328 | bytes 237353264 | solution.py:89
  456.3 7.0 copy-done
  463.3 7.9 fusion.158
  471.2 14.7 %multiply_reduce_fusion.5 = (f32[3,512]{1,0:T(4,128)S(1)}, f32[3,512,3072]{2,1,0:T(8,128)}) fusion(f32[3,512,3072]{2,1,0:T(8,128)} %copy-done, f32[3,512]{1,0:T(4,128)S(1)} %dynamic-slice_bitcast_fusion.2, pred[512,3072]{1,0:T(8,128)(4,1)S(1)} %iota_compare_fusion.5, bf16[3072,3,64]{0,2,1:T(8,128)(2,1)} %get-tuple-element.455, ...), kind=kOutput, calls=%fused_computation.18.clone.1 | convolution fusion | flops 627571200 | bytes 40710148 | tf_op jit(solution)/shard_map/while/body/eval_jaxpr/qhd,khd->hqk/dot_general | solution.py:71
  485.9 14.7 %multiply_convert_fusion.5 = bf16[3,512,3072]{2,1,0:T(8,128)(2,1)S(1)} fusion(f32[3,512,3072]{2,1,0:T(8,128)} %get-tuple-element.381, f32[3,512,3072]{2,1,0:T(8,128)} %copy-done, f32[3,512]{1,0:T(4,128)S(1)} %get-tuple-element.382, f32[3,512]{1,0:T(4,128)S(1)} %dynamic-slice_bitcast_fusion.2, pred[512,3072]{1,0:T(8,128)(4,1)S(1)} %iota_compare_fusion.5), kind=kLoop, calls=%fused_computation.17.clone.1 | loop fusion | flops 28311552 | bytes 48771072 | tf_op jit(solution)/shard_map/while/body/eval_jaxpr/convert_element_type | solution.py:76
  517.3 7.7 copy-done
  525.0 9.4 fusion.158
  534.4 14.3 %multiply_reduce_fusion.5 = (f32[3,512]{1,0:T(4,128)S(1)}, f32[3,512,3072]{2,1,0:T(8,128)}) fusion(f32[3,512,3072]{2,1,0:T(8,128)} %copy-done, f32[3,512]{1,0:T(4,128)S(1)} %dynamic-slice_bitcast_fusion.2, pred[512,3072]{1,0:T(8,128)(4,1)S(1)} %iota_compare_fusion.5, bf16[3072,3,64]{0,2,1:T(8,128)(2,1)} %get-tuple-element.455, ...), kind=kOutput, calls=%fused_computation.18.clone.1 | convolution fusion | flops 627571200 | bytes 40710148 | tf_op jit(solution)/shard_map/while/body/eval_jaxpr/qhd,khd->hqk/dot_general | solution.py:71
  548.7 14.6 %multiply_convert_fusion.5 = bf16[3,512,3072]{2,1,0:T(8,128)(2,1)S(1)} fusion(f32[3,512,3072]{2,1,0:T(8,128)} %get-tuple-element.381, f32[3,512,3072]{2,1,0:T(8,128)} %copy-done, f32[3,512]{1,0:T(4,128)S(1)} %get-tuple-element.382, f32[3,512]{1,0:T(4,128)S(1)} %dynamic-slice_bitcast_fusion.2, pred[512,3072]{1,0:T(8,128)(4,1)S(1)} %iota_compare_fusion.5), kind=kLoop, calls=%fused_computation.17.clone.1 | loop fusion | flops 28311552 | bytes 48771072 | tf_op jit(solution)/shard_map/while/body/eval_jaxpr/convert_element_type | solution.py:76
  587.4 8.8 fusion.158
  596.2 14.3 %multiply_reduce_fusion.5 = (f32[3,512]{1,0:T(4,128)S(1)}, f32[3,512,3072]{2,1,0:T(8,128)}) fusion(f32[3,512,3072]{2,1,0:T(8,128)} %copy-done, f32[3,512]{1,0:T(4,128)S(1)} %dynamic-slice_bitcast_fusion.2, pred[512,3072]{1,0:T(8,128)(4,1)S(1)} %iota_compare_fusion.5, bf16[3072,3,64]{0,2,1:T(8,128)(2,1)} %get-tuple-element.455, ...), kind=kOutput, calls=%fused_computation.18.clone.1 | convolution fusion | flops 627571200 | bytes 40710148 | tf_op jit(solution)/shard_map/while/body/eval_jaxpr/qhd,khd->hqk/dot_general | solution.py:71
  610.5 13.9 %multiply_convert_fusion.5 = bf16[3,512,3072]{2,1,0:T(8,128)(2,1)S(1)} fusion(f32[3,512,3072]{2,1,0:T(8,128)} %get-tuple-element.381, f32[3,512,3072]{2,1,0:T(8,128)} %copy-done, f32[3,512]{1,0:T(4,128)S(1)} %get-tuple-element.382, f32[3,512]{1,0:T(4,128)S(1)} %dynamic-slice_bitcast_fusion.2, pred[512,3072]{1,0:T(8,128)(4,1)S(1)} %iota_compare_fusion.5), kind=kLoop, calls=%fused_computation.17.clone.1 | loop fusion | flops 28311552 | bytes 48771072 | tf_op jit(solution)/shard_map/while/body/eval_jaxpr/convert_element_type | solution.py:76
  648.3 8.8 fusion.158
  657.1 14.3 %multiply_reduce_fusion.5 = (f32[3,512]{1,0:T(4,128)S(1)}, f32[3,512,3072]{2,1,0:T(8,128)}) fusion(f32[3,512,3072]{2,1,0:T(8,128)} %copy-done, f32[3,512]{1,0:T(4,128)S(1)} %dynamic-slice_bitcast_fusion.2, pred[512,3072]{1,0:T(8,128)(4,1)S(1)} %iota_compare_fusion.5, bf16[3072,3,64]{0,2,1:T(8,128)(2,1)} %get-tuple-element.455, ...), kind=kOutput, calls=%fused_computation.18.clone.1 | convolution fusion | flops 627571200 | bytes 40710148 | tf_op jit(solution)/shard_map/while/body/eval_jaxpr/qhd,khd->hqk/dot_general | solution.py:71
  671.4 13.9 %multiply_convert_fusion.5 = bf16[3,512,3072]{2,1,0:T(8,128)(2,1)S(1)} fusion(f32[3,512,3072]{2,1,0:T(8,128)} %get-tuple-element.381, f32[3,512,3072]{2,1,0:T(8,128)} %copy-done, f32[3,512]{1,0:T(4,128)S(1)} %get-tuple-element.382, f32[3,512]{1,0:T(4,128)S(1)} %dynamic-slice_bitcast_fusion.2, pred[512,3072]{1,0:T(8,128)(4,1)S(1)} %iota_compare_fusion.5), kind=kLoop, calls=%fused_computation.17.clone.1 | loop fusion | flops 28311552 | bytes 48771072 | tf_op jit(solution)/shard_map/while/body/eval_jaxpr/convert_element_type | solution.py:76
  709.3 8.8 fusion.158
  718.0 14.3 %multiply_reduce_fusion.5 = (f32[3,512]{1,0:T(4,128)S(1)}, f32[3,512,3072]{2,1,0:T(8,128)}) fusion(f32[3,512,3072]{2,1,0:T(8,128)} %copy-done, f32[3,512]{1,0:T(4,128)S(1)} %dynamic-slice_bitcast_fusion.2, pred[512,3072]{1,0:T(8,128)(4,1)S(1)} %iota_compare_fusion.5, bf16[3072,3,64]{0,2,1:T(8,128)(2,1)} %get-tuple-element.455, ...), kind=kOutput, calls=%fused_computation.18.clone.1 | convolution fusion | flops 627571200 | bytes 40710148 | tf_op jit(solution)/shard_map/while/body/eval_jaxpr/qhd,khd->hqk/dot_general | solution.py:71
  732.3 13.9 %multiply_convert_fusion.5 = bf16[3,512,3072]{2,1,0:T(8,128)(2,1)S(1)} fusion(f32[3,512,3072]{2,1,0:T(8,128)} %get-tuple-element.381, f32[3,512,3072]{2,1,0:T(8,128)} %copy-done, f32[3,512]{1,0:T(4,128)S(1)} %get-tuple-element.382, f32[3,512]{1,0:T(4,128)S(1)} %dynamic-slice_bitcast_fusion.2, pred[512,3072]{1,0:T(8,128)(4,1)S(1)} %iota_compare_fusion.5), kind=kLoop, calls=%fused_computation.17.clone.1 | loop fusion | flops 28311552 | bytes 48771072 | tf_op jit(solution)/shard_map/while/body/eval_jaxpr/convert_element_type | solution.py:76
  770.2 8.8 fusion.158
  779.0 14.3 %multiply_reduce_fusion.5 = (f32[3,512]{1,0:T(4,128)S(1)}, f32[3,512,3072]{2,1,0:T(8,128)}) fusion(f32[3,512,3072]{2,1,0:T(8,128)} %copy-done, f32[3,512]{1,0:T(4,128)S(1)} %dynamic-slice_bitcast_fusion.2, pred[512,3072]{1,0:T(8,128)(4,1)S(1)} %iota_compare_fusion.5, bf16[3072,3,64]{0,2,1:T(8,128)(2,1)} %get-tuple-element.455, ...), kind=kOutput, calls=%fused_computation.18.clone.1 | convolution fusion | flops 627571200 | bytes 40710148 | tf_op jit(solution)/shard_map/while/body/eval_jaxpr/qhd,khd->hqk/dot_general | solution.py:71
  793.3 13.9 %multiply_convert_fusion.5 = bf16[3,512,3072]{2,1,0:T(8,128)(2,1)S(1)} fusion(f32[3,512,3072]{2,1,0:T(8,128)} %get-tuple-element.381, f32[3,512,3072]{2,1,0:T(8,128)} %copy-done, f32[3,512]{1,0:T(4,128)S(1)} %get-tuple-element.382, f32[3,512]{1,0:T(4,128)S(1)} %dynamic-slice_bitcast_fusion.2, pred[512,3072]{1,0:T(8,128)(4,1)S(1)} %iota_compare_fusion.5), kind=kLoop, calls=%fused_computation.17.clone.1 | loop fusion | flops 28311552 | bytes 48771072 | tf_op jit(solution)/shard_map/while/body/eval_jaxpr/convert_element_type | solution.py:76
  824.1 7.0 copy.94
  831.0 143.0 %all_to_all.68 = bf16[3072,3,192]{2,1,0:T(4,128)(2,1)} all-to-all(bf16[3072,3,192]{2,1,0:T(4,128)(2,1)} %copy.94), channel_id=1, replica_groups=mesh['dp'=8,'seq'=4] {'seq'}, dimensions={0} | all-to-all | bytes 7077888 | tf_op jit(solution)/shard_map/all_to_all | solution.py:188
  974.1 10.0 copy.96
  984.1 7.3 fusion.68
  992.4 62.9 %reduce-scatter.5.cloned.1.call-done = f32[96,2304]{1,0:T(8,128)} async-done(((f32[768,2304]{1,0:T(8,128)}), f32[96,2304]{1,0:T(8,128)}) %reduce-scatter.5.cloned.1.call-update) | async-done | bytes 884752 | tf_op jit(solution)/shard_map/reduce_scatter | solution.py:200
  1055.3 10.4 fusion.66
  1068.1 8.0 fusion.98
  1084.3 25.3 %all-reduce.10 = (f32[768]{0:T(1024)S(1)}, f32[768]{0:T(1024)S(1)}, f32[768]{0:T(1024)S(1)}, f32[768]{0:T(1024)S(1)}, f32[768]{0:T(1024)S(1)}) all-reduce(f32[768]{0:T(1024)} %get-tuple-element.199, f32[768]{0:T(1024)} %get-tuple-element.198, f32[768]{0:T(1024)} %get-tuple-element.267, ...), channel_id=2, replica_groups=mesh['dp'=8,'seq'=4] {'dp'}, use_global_device_ids=true, to_apply=%region_16.17.clone | all-reduce | flops 3840 | bytes 30720
  1113.1 12.5 %all-reduce.11 = (f32[96]{0:T(128)}, f32[96]{0:T(128)}, f32[96]{0:T(128)}, f32[96]{0:T(128)}, f32[96]{0:T(128)}) all-reduce(f32[96]{0:T(128)S(1)} %dynamic-slice.6, f32[96]{0:T(128)S(1)} %dynamic-slice.8, f32[96]{0:T(128)S(1)} %dynamic-slice.10, f32[96]{0:T(128)S(1)} %dynamic-slice.12, ...), channel_id=1, replica_groups=mesh['dp'=8,'seq'=4] {'seq'}, use_global_device_ids=true, to_apply=%region_17.18 | all-reduce | flops 480 | bytes 3840 | tf_op jit(solution)/shard_map/psum | solution.py:207
  1125.7 67.4 %all-reduce.16.cloned.1.call-done = (f32[96,2304]{1,0:T(8,128)}, f32[96,768]{1,0:T(8,128)}, f32[96,3072]{1,0:T(8,128)}, f32[384,768]{1,0:T(8,128)}) async-done(((f32[96,2304]{1,0:T(8,128)}, f32[96,768]{1,0:T(8,128)}, f32[96,3072]{1,0:T(8,128)}, f32[384,768]{1,0:T(8,128)}), (f32[96,2304]{1,0:T(8,128)}, f32[96,768]{1,0:T(8,128)}, f32[96,3072]{1,0:T(8,128)}, ...) | async-done | bytes 3538960 | tf_op jit(solution)/shard_map/psum | solution.py:207
  (273 shorter events, 298.5 us)
Async XLA Ops:
  7.2 39.6 %all-gather.5.cloned.1.call-start = ((), (), s32[]{:S(2)}) async-start(), calls=%async_computation.8 | async-start | bytes 3981312 | tf_op jit(solution)/shard_map/all_gather | solution.py:117
  7.9 313.9 %all-gather.7.cloned.1.call-start = ((), (), s32[]{:S(2)}) async-start(), calls=%async_computation.9 | async-start | bytes 1327104 | tf_op jit(solution)/shard_map/all_gather | solution.py:118
  8.7 344.5 %all-gather.9.cloned.1.call-start = ((), (), s32[]{:S(2)}) async-start(), calls=%async_computation.10 | async-start | bytes 5308416 | tf_op jit(solution)/shard_map/all_gather | solution.py:121
  41.6 5.2 copy-start.38
  41.6 5.2 copy-start.23
  41.6 5.2 copy-start.28
  43.2 10.4 copy-start.2
  43.5 10.0 copy-start.26
  44.6 9.0 copy-start.30
  66.5 110.1 %all-to-all-start = ((bf16[768,3,768]{0,1,2:T(4,128)(2,1)}), bf16[768,3,768]{0,1,2:T(4,128)(2,1)}, u32[]{:S(2)}, u32[]{:S(2)}) async-start(bf16[768,3,768]{0,1,2:T(4,128)(2,1)} %copy.84), calls=%async_computation | async-start | bytes 9437184 | tf_op jit(solution)/shard_map/all_to_all | solution.py:144
  71.5 290.8 %all-gather.11.cloned.1.call-start = ((), (), s32[]{:S(2)}) async-start(), calls=%async_computation.11 | async-start | bytes 5308416 | tf_op jit(solution)/shard_map/all_gather | solution.py:122
  315.0 5.3 copy-start.41
  315.0 5.3 copy-start.40
  316.2 4.2 copy-start.15
  316.2 33.1 %copy-start.3 = (bf16[1,768,768]{1,2,0:T(8,128)(2,1)S(1)}, bf16[1,768,768]{1,2,0:T(8,128)(2,1)}, u32[]{:S(2)}) copy-start(bf16[1,768,768]{1,2,0:T(8,128)(2,1)} %copy-done.2) | copy-start | bytes 3538948
  316.2 33.1 %copy-start.24 = (f32[768]{0:T(1024)S(1)}, f32[768]{0:T(1024)}, u32[]{:S(2)}) copy-start(f32[768]{0:T(1024)} %copy-done.23) | copy-start | bytes 9220
  316.2 32.1 %all-to-all-start.1 = ((bf16[4,768,192]{1,2,0:T(8,128)(2,1)}), bf16[4,768,192]{1,2,0:T(8,128)(2,1)S(1)}, u32[]{:S(2)}, u32[]{:S(2)}) async-start(bf16[4,768,192]{1,2,0:T(8,128)(2,1)} %copy.88), calls=%async_computation.1 | async-start | bytes 2359296 | tf_op jit(solution)/shard_map/all_to_all | solution.py:153
  319.8 672.5 %reduce-scatter.7.cloned.1.call-start = ((), (), s32[]{:S(2)}) async-start(), calls=%async_computation.13 | async-start | bytes 2654208 | tf_op jit(solution)/shard_map/reduce_scatter | solution.py:201
  352.1 60.7 %copy-start.5 = (f32[768,768]{0,1:T(8,128)}, f32[768,768]{0,1:T(8,128)S(1)}, u32[]{:S(2)}) copy-start(f32[768,768]{0,1:T(8,128)S(1)} %get-tuple-element.266) | copy-start | bytes 7077892
  353.2 9.1 copy-start.16
  362.3 11.4 copy-start.13
  373.8 5.8 copy-start.42
  382.6 3.1 copy-start.35
  382.6 3.1 copy-start.7
  391.5 600.8 %reduce-scatter.11.cloned.1.call-start = ((), (), s32[]{:S(2)}) async-start(), calls=%async_computation.15 | async-start | bytes 10616832 | tf_op jit(solution)/shard_map/reduce_scatter | solution.py:205
  409.2 31.4 %all-to-all-start.2 = ((bf16[768,4,192]{0,2,1:T(8,128)(2,1)}), bf16[768,4,192]{0,2,1:T(8,128)(2,1)S(1)}, u32[]{:S(2)}, u32[]{:S(2)}) async-start(bf16[768,4,192]{0,2,1:T(8,128)(2,1)} %bitcast.185), calls=%async_computation.2 | async-start | bytes 2359296 | tf_op jit(solution)/shard_map/all_to_all | solution.py:183
  412.7 579.7 %reduce-scatter.9.cloned.1.call-start = ((), (), s32[]{:S(2)}) async-start(), calls=%async_computation.14 | async-start | bytes 10616832 | tf_op jit(solution)/shard_map/reduce_scatter | solution.py:204
  421.7 633.6 %reduce-scatter.5.cloned.1.call-start = ((), (), s32[]{:S(2)}) async-start(), calls=%async_computation.12 | async-start | bytes 7962624 | tf_op jit(solution)/shard_map/reduce_scatter | solution.py:200
  442.5 4.6 copy-start.1
  456.2 7.0 copy-start
  517.3 7.8 copy-start
  580.9 6.5 copy-start
  641.9 6.5 copy-start
  702.8 6.5 copy-start
  763.7 6.5 copy-start
  820.3 2.4 copy-start.14
  974.0 10.0 copy-start.4
  974.0 10.0 copy-start.25
  974.0 10.0 copy-start.27
  974.0 10.0 copy-start.29
  974.0 10.0 copy-start.31
  974.1 10.0 copy-start.39
  991.4 63.9 %copy-start.6 = (f32[768,768]{0,1:T(8,128)S(1)}, f32[768,768]{0,1:T(8,128)}, u32[]{:S(2)}) copy-start(f32[768,768]{0,1:T(8,128)} %copy-done.5) | copy-start | bytes 7077892
  991.4 201.6 %all-reduce.16.cloned.1.call-start = ((), (), s32[]{:S(2)}) async-start(), calls=%async_computation.16 | async-start | bytes 7077888 | tf_op jit(solution)/shard_map/psum | solution.py:207
  1078.9 2.0 copy-start.11
  1078.9 2.0 copy-start.37
  1193.0 4.0 copy-start.18
  1193.0 5.0 copy-start.17
  (12 other events, 14.6 us)
Sparse Core Ops, SparseCore 0:
  9.9 36.8 all-gather.4
  48.7 23.9 all-gather.6
  74.6 38.9 all-gather.8
  115.3 38.9 all-gather.10
  391.6 40.5 reduce-scatter.6
  436.0 76.4 reduce-scatter.10
  516.4 76.5 reduce-scatter.8
  991.6 63.6 reduce-scatter.4
  1057.9 135.0 all-reduce.15
where the time goes:
time: 1210 us
  matrix products  380 us (31%)
  waiting for transfers between devices  285 us (24%)
  blocking collectives  207 us (17%)
  other arithmetic  148 us (12%)
  local copies, waits for them, and re-layouts  137 us (11%)
  loops' own time  20.5 us (2%)
  between operations  16 us (1%)
  starting transfers between devices  13.3 us (1%)
    all_to_all x1, blocking collectives, on_device(): lax.all_to_all(grad_packed, 'seq', split_axis=0, concat_axis=2, tiled=True)  143 us
    all_to_all x1, waiting for transfers between devices, on_device(): lax.all_to_all(packed.reshape(row_count, 3, model_width), 'seq', split_ax...  105 us
    dot_general x6, matrix products, attend_back(): jnp.einsum('qhd,khd->hqk', grad_blk, values, preferred_element_type=jnp.f...  86.3 us
    convert_element_type x6, other arithmetic, attend_back(): grad_scores = (probs * (grad_probs - jnp.sum(probs * grad_probs, axis=-1,...  84.8 us
    psum x1, waiting for transfers between devices, on_device(): lax.psum((shares[0], shares[1], shares[2], shares[3], shares[4], shares[5...  67.4 us
    reduce_scatter x1, waiting for transfers between devices, on_device(): lax.psum_scatter(grad_proj_in, 'dp', scatter_dimension=0, tiled=True)  62.9 us
    dot_general x12, matrix products, causal_scores(): jnp.einsum('qhd,khd->hqk', query_blk, keys, preferred_element_type=jnp.fl...  53.3 us
    dot_general x6, matrix products, attend_back(): jnp.einsum('hqk,qhd->khd', probs_low, grad_blk, preferred_element_type=jn...  52.3 us
  transfers between devices with their start and end apart: 12, of which 6 were waited for; matrix products, arithmetic and copies ran while one was open for 48% of the time, Pallas kernels for 0%

commit v1 on v0

v1 whole, which is shorter than its diff:
```python
import functools

import jax
import jax.numpy as jnp
from jax import lax
from jax.experimental import pallas as pl
from jax.experimental.pallas import tpu as pltpu
from jax.sharding import PartitionSpec as P

HD = 64
EPSILON = 1e-05
MASKED = -1e30
F32 = jnp.float32
BF = jnp.bfloat16
MEMBERS = 4
VMEM_LIMIT = 60 << 20
GELU_A = 0.7978845608028654
GELU_B = 0.044715


def contract(left, right, left_dim, right_dim):
    return lax.dot_general(
        left, right, (((left_dim,), (right_dim,)), ((), ())), preferred_element_type=F32
    )


def normalize(hidden):
    center = hidden - jnp.mean(hidden, axis=-1, keepdims=True)
    spread = jnp.mean(center * center, axis=-1, keepdims=True)
    inverse = lax.rsqrt(spread + EPSILON)
    return center * inverse, inverse


def norm_backward(grad, gain, unit, inverse):
    scaled = grad * gain
    return inverse * (
        scaled
        - jnp.mean(scaled, axis=-1, keepdims=True)
        - unit * jnp.mean(scaled * unit, axis=-1, keepdims=True)
    )


def params(*semantics):
    return pltpu.CompilerParams(dimension_semantics=semantics, vmem_limit_bytes=VMEM_LIMIT)


def whole(shape):
    zeros = (0,) * len(shape)
    return pl.BlockSpec(shape, lambda *_: zeros, pipeline_mode=pl.Buffered(1))


def project_body(info, stay0, move0, stay1, move1, wt, *rest):
    packed, normed = rest[-2:]
    slot = pl.program_id(0)
    stay = info[0] > 0
    tokens = jnp.where(
        slot == 0,
        jnp.where(stay, stay0[...], move0[...]),
        jnp.where(stay, stay1[...], move1[...]),
    )
    width = tokens.shape[1]
    cols = wt.shape[0] - 64
    vec = wt[cols : cols + 8, :].astype(F32)
    hidden = tokens.astype(F32) + vec[0:1]
    unit, _ = normalize(hidden)
    low = (unit * vec[1:2] + vec[2:3]).astype(BF)
    normed[...] = low
    packed[...] = contract(wt[:cols, :], low, 1, 1).astype(BF)


def project(info, stay0, move0, stay1, move1, wt, carried, rows=384):
    chunk, width = stay0.shape
    cols = wt.shape[0] - 64
    length = MEMBERS * chunk
    per = chunk // rows

    def src(which):
        return pl.BlockSpec(
            (rows, width), lambda s, b, info: (jnp.where(s == which, b, which * 0 + (per - 1) * (s > which)), 0)
        )

    def place(s, b, info):
        return info[1 + s] * per + b

    in_specs = [src(0), src(0), src(1), src(1), whole(wt.shape)]
    aliases = {}
    args = [info, stay0, move0, stay1, move1, wt]
    if carried is not None:
        in_specs += [pl.BlockSpec(memory_space=pl.ANY)] * 2
        aliases = {6: 0, 7: 1}
        args += list(carried)
    return pl.pallas_call(
        project_body,
        grid_spec=pltpu.PrefetchScalarGridSpec(
            num_scalar_prefetch=1,
            grid=(2, per),
            in_specs=in_specs,
            out_specs=[
                pl.BlockSpec((cols, rows), lambda s, b, info: (0, place(s, b, info))),
                pl.BlockSpec((rows, width), lambda s, b, info: (place(s, b, info), 0)),
            ],
        ),
        out_shape=[
            jax.ShapeDtypeStruct((cols, length), BF),
            jax.ShapeDtypeStruct((length, width), BF),
        ],
        input_output_aliases=aliases,
        compiler_params=params("arbitrary", "arbitrary"),
        cost_estimate=pl.CostEstimate(
            flops=4 * chunk * width * cols, transcendentals=2 * chunk, bytes_accessed=12 * chunk * width
        ),
        name="norm_project",
    )(*args)


def diagonal(size):
    key = lax.broadcasted_iota(jnp.int32, (size, size), 0)
    query = lax.broadcasted_iota(jnp.int32, (size, size), 1)
    return key <= query


def forward_body(heads, info, packed, out0, out1, out2, out3, logsum, keys):
    step = pl.program_id(0)
    width = heads * HD
    size = out0.shape[1]
    scale = BF(HD**-0.5)

    @pl.when(step == 0)
    def _():
        for h in range(heads):
            keys[h] = packed[width + h * HD : width + (h + 1) * HD, :].T

    first = pl.multiple_of(step * size, size)
    queries = [packed[h * HD : (h + 1) * HD, pl.ds(first, size)] * scale for h in range(heads)]

    def block(start, carry, allowed):
        all_scores = [
            contract(keys[h, pl.ds(start, size), :], queries[h], 1, 0) for h in range(heads)
        ]
        result = []
        for h in range(heads):
            top, total, summed = carry[h]
            scores = all_scores[h]
            if allowed is not None:
                scores = jnp.where(allowed, scores, MASKED)
            new_top = jnp.maximum(top, jnp.max(scores, axis=0, keepdims=True))
            weights = jnp.exp(scores - new_top)
            shrink = jnp.exp(top - new_top)
            total = total * shrink + jnp.sum(weights, axis=0, keepdims=True)
            values = packed[2 * width + h * HD : 2 * width + (h + 1) * HD, pl.ds(start, size)]
            summed = summed * shrink + contract(values, weights.astype(BF), 1, 0)
            result.append((new_top, total, summed))
        return tuple(result)

    begin = tuple(
        (
            jnp.full((1, size), MASKED, F32),
            jnp.zeros((1, size), F32),
            jnp.zeros((HD, size), F32),
        )
        for _ in range(heads)
    )
    carry = lax.fori_loop(
        0, step, lambda j, c: block(pl.multiple_of(j * size, size), c, None), begin
    )
    carry = block(first, carry, diagonal(size))
    place = step ^ info[1]
    for h in range(heads):
        top, total, summed = carry[h]
        logsum[h : h + 1, :] = top + jnp.log(total)
        low = (summed / total).astype(BF)
        for j, out in enumerate((out0, out1, out2, out3)):

            @pl.when(place == j)
            def _(out=out, low=low, h=h):
                out[h * HD : (h + 1) * HD, :] = low


def attend_forward(info, packed):
    cols, length = packed.shape
    heads = cols // (3 * HD)
    width = heads * HD
    size = length // MEMBERS
    part = jax.ShapeDtypeStruct((width, size), BF)
    return pl.pallas_call(
        functools.partial(forward_body, heads),
        grid_spec=pltpu.PrefetchScalarGridSpec(
            num_scalar_prefetch=1,
            grid=(MEMBERS,),
            in_specs=[whole(packed.shape)],
            out_specs=[pl.BlockSpec((width, size), lambda s, info: (0, 0))] * MEMBERS
            + [pl.BlockSpec((8, size), lambda s, info: (0, s))],
            scratch_shapes=[pltpu.VMEM((heads, length, HD), BF)],
        ),
        out_shape=[part] * MEMBERS + [jax.ShapeDtypeStruct((8, length), F32)],
        compiler_params=params("arbitrary"),
        cost_estimate=pl.CostEstimate(
            flops=10 * heads * length * length * HD,
            transcendentals=heads * length * length // 2,
            bytes_accessed=8 * width * length,
        ),
        name="attention_forward",
    )(info, packed)


def backward_body(heads, info, packed, o0, o1, o2, o3, g0, g1, g2, g3, logsum, normed, wt, *rest):
    n0, n1, n2, n3, dw, keys, values, grad_keys, grad_values, out_all, grad_all, dw_sum = rest
    step = pl.program_id(0)
    chunk_id = MEMBERS - 1 - step
    width = heads * HD
    size = n0.shape[0]
    scale = BF(HD**-0.5)

    @pl.when(step == 0)
    def _():
        for h in range(heads):
            keys[h] = packed[width + h * HD : width + (h + 1) * HD, :].T
            values[h] = packed[2 * width + h * HD : 2 * width + (h + 1) * HD, :].T
        grad_keys[...] = jnp.zeros_like(grad_keys)
        grad_values[...] = jnp.zeros_like(grad_values)
        dw_sum[...] = jnp.zeros_like(dw_sum)
        for j, (o, g) in enumerate(((o0, g0), (o1, g1), (o2, g2), (o3, g3))):
            out_all[info[1] ^ j] = o[...]
            grad_all[info[1] ^ j] = g[...]

    first = pl.multiple_of(chunk_id * size, size)
    rows = [slice(h * HD, (h + 1) * HD) for h in range(heads)]
    query_t = [packed[r, pl.ds(first, size)] * scale for r in rows]
    query = [q.T for q in query_t]
    grad_t = [grad_all[chunk_id, r, :] for r in rows]
    grad = [g.T for g in grad_t]
    delta = [
        jnp.sum(g.astype(F32) * out_all[chunk_id, r, :].astype(F32), axis=0, keepdims=True)
        for g, r in zip(grad_t, rows)
    ]
    lse = [logsum[h : h + 1, :] for h in range(heads)]

    def block(start, carry, allowed):
        result = []
        span = pl.ds(start, size)
        for h in range(heads):
            scores = contract(keys[h, span, :], query_t[h], 1, 0)
            grad_probs = contract(values[h, span, :], grad_t[h], 1, 0)
            probs = jnp.exp(scores - lse[h])
            if allowed is not None:
                probs = jnp.where(allowed, probs, 0.0)
            grad_scores = (probs * (grad_probs - delta[h])).astype(BF)
            grad_values[h, span, :] += contract(probs.astype(BF), grad[h], 1, 0)
            grad_keys[h, span, :] += contract(grad_scores, query[h], 1, 0)
            keys_t = packed[width + h * HD : width + (h + 1) * HD, span]
            result.append(carry[h] + contract(keys_t, grad_scores, 1, 0))
        return tuple(result)

    grad_query = tuple(jnp.zeros((HD, size), F32) for _ in range(heads))
    grad_query = lax.fori_loop(
        0, chunk_id, lambda j, c: block(pl.multiple_of(j * size, size), c, None), grad_query
    )
    grad_query = block(first, grad_query, diagonal(size))
    pieces = [(g * HD**-0.5).astype(BF) for g in grad_query]
    pieces += [grad_keys[h, pl.ds(first, size), :].astype(BF).T for h in range(heads)]
    pieces += [grad_values[h, pl.ds(first, size), :].astype(BF).T for h in range(heads)]
    stacked = jnp.concatenate(pieces, axis=0)
    partial = contract(stacked, wt[: 3 * width, :], 0, 0).astype(BF)
    place = chunk_id ^ info[1]
    for j, out in enumerate((n0, n1, n2, n3)):

        @pl.when(place == j)
        def _(out=out):
            out[...] = partial

    dw_sum[...] += contract(stacked, normed[...], 1, 0)

    @pl.when(step == MEMBERS - 1)
    def _():
        dw[...] = dw_sum[...].astype(BF).T


def attend_backward(info, packed, outs, grads, logsum, normed, wt):
    cols, length = packed.shape
    heads = cols // (3 * HD)
    width = heads * HD
    size = length // MEMBERS
    model = normed.shape[1]
    last = MEMBERS - 1
    fixed = pl.BlockSpec((size, model), lambda s, info: (0, 0))
    return pl.pallas_call(
        functools.partial(backward_body, heads),
        grid_spec=pltpu.PrefetchScalarGridSpec(
            num_scalar_prefetch=1,
            grid=(MEMBERS,),
            in_specs=[whole(packed.shape)]
            + [whole((width, size))] * (2 * MEMBERS)
            + [
                pl.BlockSpec((8, size), lambda s, info: (0, last - s)),
                pl.BlockSpec((size, model), lambda s, info: (last - s, 0)),
                whole(wt.shape),
            ],
            out_specs=[fixed] * MEMBERS + [pl.BlockSpec((model, cols), lambda s, info: (0, 0))],
            scratch_shapes=[
                pltpu.VMEM((heads, length, HD), BF),
                pltpu.VMEM((heads, length, HD), BF),
                pltpu.VMEM((heads, length, HD), F32),
                pltpu.VMEM((heads, length, HD), F32),
                pltpu.VMEM((MEMBERS, width, size), BF),
                pltpu.VMEM((MEMBERS, width, size), BF),
                pltpu.VMEM((cols, model), F32),
            ],
        ),
        out_shape=[jax.ShapeDtypeStruct((size, model), BF)] * MEMBERS
        + [jax.ShapeDtypeStruct((model, cols), BF)],
        compiler_params=params("arbitrary"),
        cost_estimate=pl.CostEstimate(
            flops=20 * heads * length * length * HD,
            transcendentals=heads * length * length // 2,
            bytes_accessed=20 * width * length,
        ),
        name="attention_backward",
    )(info, packed, *outs, *grads, logsum, normed, wt)


def hidden_body(
    groups, info, tok_s, tok_m, cot_s, cot_m, m0, m1, m2, m3, vec_ref, *rest
):
    downs, ups, out_w = rest[:groups], rest[groups : 2 * groups], rest[2 * groups]
    outs = rest[2 * groups + 1 :]
    layer_out, act, grad_pre, normed, branch_grad, resid_grad, a0, a1, a2, a3, stats, cot = outs
    step = pl.program_id(0)
    stay = info[0] > 0
    member = info[1]
    vec = vec_ref[0:8, :].astype(F32)
    model = vec.shape[1]
    width = model // MEMBERS

    def square(ref):
        return ref[...].reshape(model, model)

    def out_rows(j):
        start = pl.multiple_of((member ^ j) * width, width)
        if out_w.shape[0] == 1:
            return out_w[0, pl.ds(start, width), :]
        unit = out_w.shape[1]
        return out_w[pl.ds((member ^ j) * (width // unit), width // unit)].reshape(width, model)

    tokens = jnp.where(stay, tok_s[...], tok_m[...]).astype(F32)
    cot_low = jnp.where(stay, cot_s[...], cot_m[...])
    cot[...] = cot_low
    branch_sum = None
    for j, merged in enumerate((m0, m1, m2, m3)):
        part = contract(merged[...], out_rows(j), 0, 0)
        branch_sum = part if branch_sum is None else branch_sum + part
    resid = tokens + vec[0:1] + branch_sum
    unit, inverse = normalize(resid)
    low = (unit * vec[3:4] + vec[4:5]).astype(BF)
    normed[...] = low
    result = None
    grad_n = jnp.zeros_like(resid)
    for k in range(groups):
        span = slice(k * model, (k + 1) * model)
        up, down = square(ups[k]), square(downs[k])
        pre = contract(low, up, 1, 0)
        square_pre = pre * pre
        bend = jnp.tanh(GELU_A * pre * (1.0 + GELU_B * square_pre))
        half = 0.5 + 0.5 * bend
        act_low = (pre * half).astype(BF)
        act[:, span] = act_low
        part = contract(act_low, down, 1, 0)
        result = part if result is None else result + part
        slope = half + 0.5 * pre * (1.0 - bend * bend) * (
            GELU_A * (1.0 + 3.0 * GELU_B * square_pre)
        )
        grad_low = (contract(cot_low, down, 1, 1) * slope).astype(BF)
        grad_pre[:, span] = grad_low
        grad_n = grad_n + contract(grad_low, up, 1, 1)
    layer_out[...] = (resid + result).astype(BF)
    grad_resid = cot_low.astype(F32) + norm_backward(grad_n, vec[3:4], unit, inverse)
    resid_grad[...] = grad_resid
    branch = grad_resid.astype(BF)
    branch_grad[...] = branch
    for j, out in enumerate((a0, a1, a2, a3)):
        out[...] = contract(out_rows(j), branch, 1, 1).astype(BF)

    @pl.when(step == 0)
    def _():
        stats[...] = jnp.zeros_like(stats)

    stats[0:1, :] += jnp.sum(grad_n * unit, axis=0, keepdims=True)
    stats[1:2, :] += jnp.sum(grad_n, axis=0, keepdims=True)


def weight_specs(weights, groups):
    split, height, model = weights.shape
    unit = model // split
    tall = height - (groups + 1) * unit
    one = pl.Buffered(1)
    per = model // tall if tall < model else 1
    if split == 1:
        specs = [
            pl.BlockSpec((1, model, model), lambda s, info, k=k: (0, k, 0), pipeline_mode=one)
            for k in range(2 * groups + 1)
        ]
        return specs
    downs = [
        pl.BlockSpec((per, tall, model), lambda s, info, k=k: (k, 0, 0), pipeline_mode=one)
        for k in range(groups)
    ]
    base = tall // unit
    others = [
        pl.BlockSpec((split, unit, model), lambda s, info, k=k: (0, base + k, 0), pipeline_mode=one)
        for k in range(groups + 1)
    ]
    return downs + others


def hidden_layer(info, tok_s, tok_m, cot_s, cot_m, merged, wt, weights, groups, rows=256):
    size, model = tok_s.shape
    width = model // MEMBERS
    hidden = groups * model
    tok = pl.BlockSpec((rows, model), lambda s, info: (s, 0))
    col = pl.BlockSpec((width, rows), lambda s, info: (0, s))
    wide = pl.BlockSpec((rows, hidden), lambda s, info: (s, 0))
    vec_block = wt.shape[0] // 64 - 1
    n_weights = 2 * groups + 1

    def shaped(shape, dtype):
        return jax.ShapeDtypeStruct(shape, dtype)

    return pl.pallas_call(
        functools.partial(hidden_body, groups),
        grid_spec=pltpu.PrefetchScalarGridSpec(
            num_scalar_prefetch=1,
            grid=(size // rows,),
            in_specs=[tok] * 4
            + [col] * MEMBERS
            + [pl.BlockSpec((64, model), lambda s, info: (vec_block, 0))]
            + weight_specs(weights, groups),
            out_specs=[tok, wide, wide, tok, tok, tok]
            + [col] * MEMBERS
            + [pl.BlockSpec((8, model), lambda s, info: (0, 0)), tok],
        ),
        out_shape=[
            shaped((size, model), BF),
            shaped((size, hidden), BF),
            shaped((size, hidden), BF),
            shaped((size, model), BF),
            shaped((size, model), BF),
            shaped((size, model), F32),
        ]
        + [shaped((width, size), BF)] * MEMBERS
        + [shaped((8, model), F32), shaped((size, model), BF)],
        compiler_params=params("arbitrary"),
        cost_estimate=pl.CostEstimate(
            flops=2 * size * model * (4 * hidden + 2 * model),
            transcendentals=size * hidden,
            bytes_accessed=2 * weights.size + 24 * size * model,
        ),
        name="hidden_layer",
    )(info, tok_s, tok_m, cot_s, cot_m, *merged, wt, *([weights] * n_weights))


def grads_body(groups, info, act, grad_pre, normed, branch, cot, m0, m1, m2, m3, out, stage, sems):
    step = pl.program_id(0)
    slot = step % 2
    member = info[1]
    units = stage.shape[1]
    unit = stage.shape[2]
    model = stage.shape[3]
    split, height, _ = out.shape
    tall = height - (groups + 1) * (model // split)

    def drain(which):
        pltpu.make_async_copy(stage.at[which], stage.at[which], sems.at[which]).wait()

    @pl.when(step >= 2)
    def _():
        drain(slot)

    @pl.when(step < groups)
    def _():
        stage[slot] = contract(act[...], cot[...], 0, 0).astype(BF).reshape(units, unit, model)

    @pl.when(jnp.logical_and(step >= groups, step < 2 * groups))
    def _():
        stage[slot] = (
            contract(normed[...], grad_pre[...], 0, 0).astype(BF).reshape(units, unit, model)
        )

    @pl.when(step == 2 * groups)
    def _():
        share = units // MEMBERS
        for j, merged in enumerate((m0, m1, m2, m3)):
            piece = contract(merged[...], branch[...], 1, 0).astype(BF)
            stage[slot, pl.ds((member ^ j) * share, share)] = piece.reshape(share, unit, model)

    for b in range(units):
        if split == 1:
            row, start = 0, step * model + b * unit
        else:
            per = tall // unit
            flat = step * units + b
            is_down = step < groups
            row = jnp.where(is_down, flat // per, b)
            start = jnp.where(is_down, (flat % per) * unit, tall + (step - groups) * unit)
        start = pl.multiple_of(start, 16)
        pltpu.make_async_copy(
            stage.at[slot, b], out.at[row, pl.ds(start, unit), :], sems.at[slot]
        ).start()

    @pl.when(step == 2 * groups)
    def _():
        drain(1 - slot)
        drain(slot)


def weight_grads(info, act, grad_pre, normed, branch, cot, merged, split, groups):
    size, model = normed.shape
    width = model // MEMBERS
    units = 8
    height = (2 * groups + 1) * (model // split)
    return pl.pallas_call(
        functools.partial(grads_body, groups),
        grid_spec=pltpu.PrefetchScalarGridSpec(
            num_scalar_prefetch=1,
            grid=(2 * groups + 1,),
            in_specs=[
                pl.BlockSpec((size, model), lambda s, info: (0, jnp.minimum(s, groups - 1))),
                pl.BlockSpec(
                    (size, model), lambda s, info: (0, jnp.clip(s - groups, 0, groups - 1))
                ),
                whole((size, model)),
                whole((size, model)),
                whole((size, model)),
            ]
            + [whole((width, size))] * MEMBERS,
            out_specs=pl.BlockSpec(memory_space=pl.ANY),
            scratch_shapes=[
                pltpu.VMEM((2, units, model // units, model), BF),
                pltpu.SemaphoreType.DMA((2,)),
            ],
        ),
        out_shape=jax.ShapeDtypeStruct((split, height, model), BF),
        compiler_params=params("arbitrary"),
        cost_estimate=pl.CostEstimate(
            flops=2 * size * model * model * (2 * groups + 1),
            transcendentals=0,
            bytes_accessed=2 * (2 * groups + 1) * model * (model + size),
        ),
        name="weight_grads",
    )(info, act, grad_pre, normed, branch, cot, *merged)


def final_body(info, tok_s, tok_m, p0, p1, p2, resid_grad, vec_ref, before, out, low, stats):
    step = pl.program_id(0)
    stay = info[0] > 0
    vec = vec_ref[0:8, :].astype(F32)
    tokens = jnp.where(stay, tok_s[...], tok_m[...]).astype(F32)
    unit, inverse = normalize(tokens + vec[0:1])
    grad = p0[...].astype(F32) + p1[...].astype(F32) + p2[...].astype(F32)
    result = resid_grad[...] + norm_backward(grad, vec[1:2], unit, inverse)
    out[...] = result
    low[...] = result.astype(BF)

    @pl.when(step == 0)
    def _():
        stats[...] = before[...]

    stats[2:3, :] += jnp.sum(grad * unit, axis=0, keepdims=True)
    stats[3:4, :] += jnp.sum(grad, axis=0, keepdims=True)
    stats[4:5, :] += jnp.sum(result, axis=0, keepdims=True)


def final_norm(info, tok_s, tok_m, parts, resid_grad, wt, before, rows=256):
    size, model = tok_s.shape
    tok = pl.BlockSpec((rows, model), lambda s, info: (s, 0))
    one = pl.BlockSpec((8, model), lambda s, info: (0, 0))
    vec_block = wt.shape[0] // 64 - 1
    return pl.pallas_call(
        final_body,
        grid_spec=pltpu.PrefetchScalarGridSpec(
            num_scalar_prefetch=1,
            grid=(size // rows,),
            in_specs=[tok] * 6 + [pl.BlockSpec((64, model), lambda s, info: (vec_block, 0)), one],
            out_specs=[tok, tok, one],
        ),
        out_shape=[
            jax.ShapeDtypeStruct((size, model), F32),
            jax.ShapeDtypeStruct((size, model), BF),
            jax.ShapeDtypeStruct((8, model), F32),
        ],
        compiler_params=params("arbitrary"),
        cost_estimate=pl.CostEstimate(
            flops=30 * size * model, transcendentals=size, bytes_accessed=20 * size * model
        ),
        name="final_norm",
    )(info, tok_s, tok_m, *parts, resid_grad, wt, before)


def after(value, *others):
    return lax.optimization_barrier((value, *others))[0]


def on_device(
    groups_dp,
    inputs,
    pass_embed,
    gain_attend,
    shift_attend,
    attend_in,
    attend_out,
    gain_hidden,
    shift_hidden,
    hidden_up,
    hidden_down,
    cotangent,
):
    axes = ("dp", "seq")
    dp = groups_dp
    row = lax.axis_index("dp")
    line = lax.axis_index("seq")
    core = row & 1
    stays = core == (line >> 1)
    member = core * 2 + (line & 1)
    model = inputs.shape[2]
    width = model // MEMBERS
    share = attend_in.shape[0]
    groups = hidden_up.shape[1] // model

    def send(value, target):
        pairs = []
        for d in range(dp):
            for z in range(MEMBERS):
                goal = target(d, z)
                if goal is not None:
                    pairs.append((d * MEMBERS + z, goal[0] * MEMBERS + goal[1]))
        return lax.ppermute(value, axes, pairs)

    def at_home(d, z):
        return (d & 1) == (z >> 1)

    def swap(d, z):
        return None if at_home(d, z) else (d ^ 1, z ^ 2)

    def other_core(d, z):
        return (d ^ 1, z)

    def next_chip(d, z):
        return (d, z ^ 1)

    mine = inputs[0]
    first = send(mine, lambda d, z: (d, z ^ 1) if at_home(d, z) else (d ^ 1, z ^ 2))
    mine_other = send(mine, other_core)
    late = send(first, lambda d, z: None if at_home(d, z) else (d, z ^ 1))
    first_other = send(first, other_core)
    late_other = send(late, other_core)

    columns = attend_in.reshape(share, 3, MEMBERS, width).transpose(2, 0, 1, 3)
    columns = columns.reshape(MEMBERS, share, 3 * width)
    vectors = jnp.stack([pass_embed, gain_attend, shift_attend, gain_hidden, shift_hidden], axis=1)
    vectors = jnp.pad(vectors, ((0, 0), (0, 59)))

    def for_member(which):
        piece = lax.dynamic_index_in_dim(columns, which, 0, keepdims=False)
        return jnp.concatenate([piece, vectors], axis=1)

    gathered = for_member(member)[None]
    received = send(for_member(member ^ 2), other_core)[None]
    bit = 0
    while True:
        upper = ((row >> bit) & 1) == 1
        gathered = jnp.where(
            upper,
            jnp.concatenate([received, gathered]),
            jnp.concatenate([gathered, received]),
        )
        bit += 1
        if (1 << bit) >= dp:
            break
        received = send(gathered, lambda d, z, bit=bit: (d ^ (1 << bit), z))
    wt = gathered.reshape(model, 3 * width + 64).T

    pack = jnp.concatenate(
        [hidden_down]
        + [hidden_up[:, k * model : (k + 1) * model] for k in range(groups)]
        + [attend_out]
    )
    height = pack.shape[0]
    weights = lax.all_gather(pack, "dp", axis=0, tiled=False)
    split = dp if (model // dp) % 96 == 0 else 1
    if split == 1:
        tall = hidden_down.shape[0]
        down = weights[:, :tall].reshape(1, dp * tall, model)
        others = weights[:, tall:].reshape(dp, groups + 1, share, model).transpose(1, 0, 2, 3)
        weights = jnp.concatenate([down, others.reshape(1, -1, model)], axis=1)

    stay_flag = stays.astype(jnp.int32)
    early = jnp.where(stays, member, member ^ 2)
    info = jnp.stack([stay_flag, member, member, member]).astype(jnp.int32)
    info_early = jnp.stack([stay_flag, early, early ^ 1]).astype(jnp.int32)
    info_late = jnp.stack([stay_flag, early ^ 2, early ^ 3]).astype(jnp.int32)
    carried = project(info_early, mine, mine_other, first, first_other, wt, None)
    packed, normed = project(info_late, first_other, first, late_other, late, wt, carried)

    *outs, logsum = attend_forward(info, packed)
    routes = [None, next_chip, other_core, lambda d, z: (d ^ 1, z ^ 1)]
    merged = [outs[0]] + [send(outs[j], routes[j]) for j in (1, 3, 2)]
    merged = [merged[0], merged[1], merged[3], merged[2]]

    grad_mine = cotangent[0]
    grad_moved = send(after(grad_mine, late), swap)
    (
        layer_out,
        act,
        grad_pre,
        normed_two,
        branch,
        resid_grad,
        a0,
        a1,
        a2,
        a3,
        stats,
        cot,
    ) = hidden_layer(
        info, mine, first, grad_mine, grad_moved, merged, wt, weights, groups
    )
    r1 = send(a1, routes[1])
    r3 = send(a3, routes[3])
    r2 = send(a2, routes[2])
    grads = weight_grads(info, act, grad_pre, normed_two, branch, cot, merged, split, groups)
    if split == 1:
        tall = hidden_down.shape[0]
        down = grads[0, : dp * tall].reshape(dp, tall, model)
        others = grads[0, dp * tall :].reshape(groups + 1, dp, share, model).transpose(1, 0, 2, 3)
        grads = jnp.concatenate([down, others.reshape(dp, -1, model)], axis=1)
    reduced = lax.psum_scatter(grads, "dp", scatter_dimension=0, tiled=True)[0]
    total = lax.psum(reduced, "seq").astype(F32)

    layer_moved = send(after(layer_out, r3), swap)
    n0, n1, n2, n3, dw = attend_backward(
        info, packed, outs, [a0, r1, r2, r3], logsum, normed, wt
    )
    c3 = send(n3, other_core)
    c2 = send(n2, other_core)
    partial = (n1.astype(F32) + c3.astype(F32)).astype(BF)
    z1 = send(partial, next_chip)
    input_grad, input_low, stats = final_norm(
        info, mine, first, [n0, c2, z1], resid_grad, wt, stats
    )
    input_moved = send(input_low, swap)

    current = dw.reshape(dp, share, 3 * width)
    bit = dp.bit_length() - 2
    while bit > 0:
        half = current.shape[0] // 2
        upper = ((row >> bit) & 1) == 1
        give = jnp.where(upper, current[:half], current[half:])
        keep = jnp.where(upper, current[half:], current[:half])
        got = send(give, lambda d, z, bit=bit: (d ^ (1 << bit), z))
        current = (keep.astype(F32) + got.astype(F32)).astype(BF)
        bit -= 1
    got = send(current, lambda d, z: (d, z ^ 2))
    current = (current.astype(F32) + got.astype(F32)).astype(BF)
    upper = core == 1
    give = jnp.where(upper, current[0], current[1])
    keep = jnp.where(upper, current[1], current[0])
    got = send(give, other_core)
    pair = jnp.where(upper, jnp.stack([got, keep]), jnp.stack([keep, got]))
    far = send(pair, next_chip)
    odd = (line & 1) == 1
    quad = jnp.where(odd, jnp.stack([far, pair], axis=1), jnp.stack([pair, far], axis=1))
    proj_grad = quad.reshape(MEMBERS, share, 3, width).transpose(1, 2, 0, 3)
    proj_grad = proj_grad.reshape(share, 3 * model).astype(F32)

    for flip in [lambda d, z, b=b: (d ^ (1 << b), z) for b in range(dp.bit_length() - 1)] + [
        lambda d, z: (d, z ^ 1),
        lambda d, z: (d, z ^ 2),
    ]:
        stats = stats + send(stats, flip)
    small = lax.dynamic_slice(stats, (0, row * share), (8, share))

    tall = hidden_down.shape[0]
    down_grad = total[:tall]
    up_grad = jnp.concatenate(
        [total[tall + k * share : tall + (k + 1) * share] for k in range(groups)], axis=1
    )
    out_grad = total[tall + groups * share :]
    return (
        jnp.where(stays, layer_out, layer_moved)[None],
        jnp.where(stays, input_grad, input_moved.astype(F32))[None],
        small[4],
        small[2],
        small[3],
        proj_grad,
        out_grad,
        small[0],
        small[1],
        up_grad,
        down_grad,
    )


def solution(mesh):
    vector, matrix, tokens = P("dp"), P("dp", None), P("dp", "seq", None)
    return jax.shard_map(
        functools.partial(on_device, mesh.shape["dp"]),
        mesh=mesh,
        in_specs=(
            tokens,
            vector,
            vector,
            vector,
            matrix,
            matrix,
            vector,
            vector,
            matrix,
            matrix,
            tokens,
        ),
        out_specs=(
            tokens,
            tokens,
            vector,
            vector,
            vector,
            matrix,
            matrix,
            vector,
            vector,
            matrix,
            matrix,
        ),
        check_vma=False,
    )
```

time: 1210 us -> 457 us (0.38)
  matrix products: 380 us -> 0 us
  blocking collectives: 207 us -> 0 us
  Pallas kernels: 0 us -> 168 us
  other arithmetic: 148 us -> 21.8 us
  waiting for transfers between devices: 285 us -> 164 us
  local copies, waits for them, and re-layouts: 137 us -> 20.2 us
  starting transfers between devices: 13.3 us -> 59.9 us
  loops' own time: 20.5 us -> 0 us
    dot_general x54 -> x0, matrix products: 380 us -> none  [the longest x6 86.3 us: attend_back(): jnp.einsum('qhd,khd->hqk', grad_blk, values, preferred_element_type=jnp.f...]
    pallas_call x0 -> x7, Pallas kernels: none -> 168 us  [the longest x1 66.4 us: attend_backward(): pl.pallas_call(functools.partial(backward_body, heads), grid_spec=pltpu.P...]
    all_to_all x3 -> x0, waiting for transfers between devices: 150 us -> none  [the longest x1 105 us: on_device(): lax.all_to_all(packed.reshape(row_count, 3, model_width), 'seq', split_ax...]
    all_to_all x1 -> x0, blocking collectives: 143 us -> none  [on_device(): lax.all_to_all(grad_packed, 'seq', split_axis=0, concat_axis=2, tiled=True)]
    ppermute x0 -> x30, waiting for transfers between devices: none -> 143 us  [send(): return lax.ppermute(value, axes, pairs)]
    convert_element_type x14 -> x5, other arithmetic: 87.2 us -> 2.46 us  [the longest x1 1.12 us: on_device(): current = (current.astype(F32) + got.astype(F32)).astype(BF)]
    reduce_scatter x4 -> x1, waiting for transfers between devices: 63 us -> 0.01 us  [on_device(): reduced = lax.psum_scatter(grads, 'dp', scatter_dimension=0, tiled=True)[0]]
    ppermute x0 -> x30, starting transfers between devices: none -> 59.8 us  [send(): return lax.ppermute(value, axes, pairs)]
  transfers between devices with their start and end apart: 12 -> 33, of which waited for: 6 -> 17; matrix products, arithmetic and copies ran while one was open for 48% -> 7% of each run, Pallas kernels for 0% -> 27%
where the time goes in v1:
time: 457 us; the launch traced here: 448 us
  Pallas kernels  168 us (37%)
  waiting for transfers between devices  164 us (36%)
  starting transfers between devices  59.9 us (13%)
  other arithmetic  21.8 us (5%)
  local copies, waits for them, and re-layouts  20.2 us (4%)
  between operations  14.6 us (3%)
    ppermute x30, waiting for transfers between devices, send(): return lax.ppermute(value, axes, pairs)  143 us
    pallas_call x1, Pallas kernels, attend_backward(): pl.pallas_call(functools.partial(backward_body, heads), grid_spec=pltpu.P...  66.4 us
    ppermute x30, starting transfers between devices, send(): return lax.ppermute(value, axes, pairs)  59.8 us
    pallas_call x1, Pallas kernels, hidden_layer(): pl.pallas_call(functools.partial(hidden_body, groups), grid_spec=pltpu.Pr...  31.3 us
    pallas_call x1, Pallas kernels, attend_forward(): pl.pallas_call(functools.partial(forward_body, heads), grid_spec=pltpu.Pr...  29.1 us
    psum x1, waiting for transfers between devices, on_device(): total = lax.psum(reduced, 'seq').astype(F32)  20.8 us
    pallas_call x1, Pallas kernels, weight_grads(): pl.pallas_call(functools.partial(grads_body, groups), grid_spec=pltpu.Pre...  17 us
    pallas_call x2, Pallas kernels, project(): pl.pallas_call(project_body, grid_spec=pltpu.PrefetchScalarGridSpec(num_s...  16.9 us
  transfers between devices with their start and end apart: 33, of which 17 were waited for; matrix products, arithmetic and copies ran while one was open for 7% of the time, Pallas kernels for 27%

profile of v1, /device:TPU:0, one launch (start us, length us, event | category | flops | bytes accessed | tf_op | source)
XLA Modules:
  0.0 448.4 jit_solution(13684941216976373646)
XLA Ops:
  10.2 3.0 collective-permute-start
  13.2 26.7 %collective-permute-done.stay1.move0.tok_m = bf16[768,768]{1,0:T(8,128)(2,1)S(1)} collective-permute-done((bf16[768,768]{1,0:T(8,128)(2,1)S(1)}, bf16[768,768]{1,0:T(8,128)(2,1)S(1)}, u32[]{:S(2)}, u32[]{:S(2)}) %collective-permute-start) | collective-permute-done | bytes 1179680 | tf_op jit(solution)/shard_map/ppermute | solution.py:634
  39.9 1.7 collective-permute-start.1
  42.4 1.6 reshape.111
  45.2 1.5 fusion.3
  46.7 1.9 collective-permute-start.5
  49.2 8.2 %collective-permute-start.4 = (bf16[768,768]{1,0:T(8,128)(2,1)}, bf16[768,768]{1,0:T(8,128)(2,1)}, u32[]{:S(2)}, u32[]{:S(2)}) collective-permute-start(bf16[768,768]{1,0:T(8,128)(2,1)} %collective-permute-done.1.move1), channel_id=1, source_target_pairs={{0,4},{1,5},{2,6},{3,7},{4,0},{5,1},{6,2},{7,3},{8,12},{9,13},{10,... | collective-permute-start | bytes 3538952 | tf_op jit(solution)/shard_map/ppermute | solution.py:634
  57.4 1.8 maximum_select_fusion.3
  59.2 1.5 collective-permute-start.6
  60.7 12.6 %collective-permute-done.6 = bf16[2,96,640]{2,1,0:T(8,128)(2,1)} collective-permute-done((bf16[2,96,640]{2,1,0:T(8,128)(2,1)}, bf16[2,96,640]{2,1,0:T(8,128)(2,1)}, u32[]{:S(2)}, u32[]{:S(2)}) %collective-permute-start.6) | collective-permute-done | bytes 245792 | tf_op jit(solution)/shard_map/ppermute | solution.py:634
  73.3 2.2 maximum_select_fusion.1
  75.5 1.5 collective-permute-start.7
  78.8 9.3 %collective-permute-done.7 = bf16[4,96,640]{2,1,0:T(8,128)(2,1)} collective-permute-done((bf16[4,96,640]{2,1,0:T(8,128)(2,1)}, bf16[4,96,640]{2,1,0:T(8,128)(2,1)}, u32[]{:S(2)}, u32[]{:S(2)}) %collective-permute-start.7) | collective-permute-done | bytes 491552 | tf_op jit(solution)/shard_map/ppermute | solution.py:634
  88.1 2.7 maximum_select_fusion
  90.8 2.3 copy.55
  93.0 1.8 collective-permute-start.2
  95.8 8.4 %norm_project.2 = (bf16[576,3072]{1,0:T(8,128)(2,1)}, bf16[3072,768]{1,0:T(8,128)(2,1)}) custom-call(s32[3]{0:T(128)} %pad_add_fusion.2.info, bf16[768,768]{1,0:T(8,128)(2,1)} %bitcast.65, bf16[768,768]{1,0:T(8,128)(2,1)} %collective-permute-done.8.move0, bf16[768,768]{1,0:T(8,128)(2,1)} %copy-done, bf16[768,768]{1,0:T(8,128)(2,1)} %copy-done.3, ...), custom_call_target="tpu_custom_call" | custom-call | flops 1358954496 | bytes 7077888 | tf_op jit(solution)/shard_map/norm_project/pallas_call | solution.py:92
  104.2 8.5 %norm_project.3 = (bf16[576,3072]{1,0:T(8,128)(2,1)}, bf16[3072,768]{1,0:T(8,128)(2,1)}) custom-call(s32[3]{0:T(128)} %pad_add_fusion.1.info, bf16[768,768]{1,0:T(8,128)(2,1)} %copy-done.3, bf16[768,768]{1,0:T(8,128)(2,1)} %copy-done, bf16[768,768]{1,0:T(8,128)(2,1)} %collective-permute-done.4.stay1, ...), custom_call_target="tpu_custom_call", output_to_operand_aliasing={{0}: (6, {}), {1}: (7, {})} | custom-call | flops 1358954496 | bytes 7077888 | tf_op jit(solution)/shard_map/norm_project/pallas_call | solution.py:92
  112.7 29.1 %attention_forward.1 = (bf16[192,768]{1,0:T(8,128)(2,1)}, bf16[192,768]{1,0:T(8,128)(2,1)}, bf16[192,768]{1,0:T(8,128)(2,1)}, bf16[192,768]{1,0:T(8,128)(2,1)}, f32[8,3072]{1,0:T(8,128)}) custom-call(s32[4]{0:T(128)} %pad_add_fusion.info, bf16[576,3072]{1,0:T(8,128)(2,1)} %get-tuple-element.45.packed), custom_call_target="tpu_custom_call" | custom-call | flops 18119393280 | bytes 4718592 | tf_op jit(solution)/shard_map/attention_forward/pallas_call | solution.py:185
  141.8 1.7 collective-permute-start.9
  143.5 4.7 %collective-permute-start.10 = (bf16[192,768]{1,0:T(8,128)(2,1)}, bf16[192,768]{1,0:T(8,128)(2,1)S(1)}, u32[]{:S(2)}, u32[]{:S(2)}) collective-permute-start(bf16[192,768]{1,0:T(8,128)(2,1)} %get-tuple-element.48.o2), channel_id=1, source_target_pairs={{0,4},{1,5},{2,6},{3,7},{4,0},{5,1},{6,2},{7,3},{8,12},{9,13},{10,... | collective-permute-start | bytes 884744 | tf_op jit(solution)/shard_map/ppermute | solution.py:634
  149.6 9.4 %collective-permute-done.11.m3 = bf16[192,768]{1,0:T(8,128)(2,1)S(1)} collective-permute-done((bf16[192,768]{1,0:T(8,128)(2,1)}, bf16[192,768]{1,0:T(8,128)(2,1)S(1)}, u32[]{:S(2)}, u32[]{:S(2)}) %collective-permute-start.11) | collective-permute-done | bytes 294944 | tf_op jit(solution)/shard_map/ppermute | solution.py:634
  159.7 31.3 %hidden_layer.1 = (bf16[768,768]{1,0:T(8,128)(2,1)}, bf16[768,3072]{1,0:T(8,128)(2,1)}, bf16[768,3072]{1,0:T(8,128)(2,1)}, bf16[768,768]{1,0:T(8,128)(2,1)}, bf1...) custom-call(s32[4]{0:T(128)} %pad_add_fusion.info, ...), custom_call_target="tpu_custom_call" | custom-call | flops 16307453952 | bytes 24772608 | tf_op jit(solution)/shard_map/hidden_layer/pallas_call | solution.py:427
  191.0 17.0 %weight_grads.1 = bf16[8,864,768]{2,1,0:T(8,128)(2,1)} custom-call(s32[4]{0:T(128)} %pad_add_fusion.info, bf16[768,3072]{1,0:T(8,128)(2,1)} %get-tuple-element.68.act, bf16[768,3072]{1,0:T(8,128)(2,1)} %get-tuple-element.69.grad_pre, bf16[768,768]{1,0:T(8,128)(2,1)} %get-tuple-element.70.normed, bf16[768,768]{1,0:T(8,128)(2,1)} %get-tuple-element.71.branch, ...), custom_call_target="tpu_custom_call" | custom-call | flops 8153726976 | bytes 21233664 | tf_op jit(solution)/shard_map/weight_grads/pallas_call | solution.py:519
  209.1 1.7 collective-permute-start.14
  210.9 7.1 %collective-permute-done.12.g3 = bf16[192,768]{1,0:T(8,128)(2,1)S(1)} collective-permute-done((bf16[192,768]{1,0:T(8,128)(2,1)S(1)}, bf16[192,768]{1,0:T(8,128)(2,1)S(1)}, u32[]{:S(2)}, u32[]{:S(2)}) %collective-permute-start.12) | collective-permute-done | bytes 294944 | tf_op jit(solution)/shard_map/ppermute | solution.py:634
  218.0 6.6 %collective-permute-done.14.g1 = bf16[192,768]{1,0:T(8,128)(2,1)S(1)} collective-permute-done((bf16[192,768]{1,0:T(8,128)(2,1)S(1)}, bf16[192,768]{1,0:T(8,128)(2,1)S(1)}, u32[]{:S(2)}, u32[]{:S(2)}) %collective-permute-start.14) | collective-permute-done | bytes 294944 | tf_op jit(solution)/shard_map/ppermute | solution.py:634
  225.4 66.4 %attention_backward.1 = (bf16[768,768]{1,0:T(8,128)(2,1)}, bf16[768,768]{1,0:T(8,128)(2,1)}, bf16[768,768]{1,0:T(8,128)(2,1)}, bf16[768,768]{1,0:T(8,128)(2,1)}, bf16[768,576]{1,0:T(8,128)(2,1)}) custom-call(s32[4]{0:T(128)} %pad_add_fusion.info, bf16[576,3072]{1,0:T(8,128)(2,1)} %get-tuple-element.45.packed, bf16[192,768]{1,0:T(8,128)(2,1)} %get-tuple-element.46.m0.o0, ...), custom_call_target="tpu_custom_call" | custom-call | flops 36238786560 | bytes 11796480 | tf_op jit(solution)/shard_map/attention_backward/pallas_call | solution.py:286
  291.9 1.4 broadcast_select_fusion
  293.3 1.6 collective-permute-start.25
  295.8 11.1 %collective-permute-done.25 = bf16[4,96,576]{2,1,0:T(8,128)(2,1)S(1)} collective-permute-done((bf16[4,96,576]{2,1,0:T(8,128)(2,1)S(1)}, bf16[4,96,576]{2,1,0:T(8,128)(2,1)S(1)}, u32[]{:S(2)}, u32[]{:S(2)}) %collective-permute-start.25) | collective-permute-done | bytes 442400 | tf_op jit(solution)/shard_map/ppermute | solution.py:634
  307.1 1.6 collective-permute-start.26
  308.7 1.7 collective-permute-start.13
  310.4 4.4 collective-permute-done.26
  315.5 1.3 collective-permute-start.27
  316.8 33.2 %collective-permute-done.27 = bf16[2,96,576]{2,1,0:T(8,128)(2,1)} collective-permute-done((bf16[2,96,576]{2,1,0:T(8,128)(2,1)}, bf16[2,96,576]{2,1,0:T(8,128)(2,1)}, u32[]{:S(2)}, u32[]{:S(2)}) %collective-permute-start.27) | collective-permute-done | bytes 221216 | tf_op jit(solution)/shard_map/ppermute | solution.py:634
  352.2 7.6 %final_norm.1 = (f32[768,768]{1,0:T(8,128)}, bf16[768,768]{1,0:T(8,128)(2,1)}, f32[8,768]{1,0:T(8,128)}) custom-call(s32[4]{0:T(128)} %pad_add_fusion.info, bf16[768,768]{1,0:T(8,128)(2,1)} %bitcast.67, bf16[768,768]{1,0:T(8,128)(2,1)} %copy-done, bf16[768,768]{1,0:T(8,128)(2,1)} %get-tuple-element.58.p0, bf16[768,768]{1,0:T(8,128)(2,1)} %copy-done.7, ...), custom_call_target="tpu_custom_call" | custom-call | flops 17694720 | bytes 11796480 | tf_op jit(solution)/shard_map/final_norm/pallas_call | solution.py:576
  361.5 1.3 collective-permute-done.20
  364.3 3.1 collective-permute-done.21
  367.4 1.5 collective-permute-start.22
  369.0 2.3 collective-permute-done.22
  372.4 9.9 %collective-permute-done.23 = f32[8,768]{1,0:T(8,128)S(1)} collective-permute-done((f32[8,768]{1,0:T(8,128)S(1)}, f32[8,768]{1,0:T(8,128)S(1)}, u32[]{:S(2)}, u32[]{:S(2)}) %collective-permute-start.23) | collective-permute-done | bytes 24608 | tf_op jit(solution)/shard_map/ppermute | solution.py:634
  382.9 20.7 %collective-permute-start.24 = (f32[8,768]{1,0:T(8,128)}, f32[8,768]{1,0:T(8,128)}, u32[]{:S(2)}, u32[]{:S(2)}) collective-permute-start(f32[8,768]{1,0:T(8,128)} %add.53), channel_id=1, source_target_pairs={{0,2},{1,3},{2,0},{3,1},{4,6},{5,7},{6,4},{7,5},{8,10},{9,11},{10,... | collective-permute-start | bytes 73736 | tf_op jit(solution)/shard_map/ppermute | solution.py:634
  405.0 1.7 reshape.115
  406.7 4.3 collective-permute-done.24
  412.3 3.4 select_bitcast_fusion
  415.7 20.8 %all-reduce.3.cloned.1.call-done = bf16[864,768]{1,0:T(8,128)(2,1)} async-done(((bf16[864,768]{1,0:T(8,128)(2,1)}), bf16[864,768]{1,0:T(8,128)(2,1)}) %all-reduce.3.cloned.1.call-update) | async-done | bytes 1327120 | tf_op jit(solution)/shard_map/psum | solution.py:735
  436.6 2.0 fusion.6
  (121 shorter events, 26.7 us)
Async XLA Ops:
  7.2 1.4 copy-start.12
  7.2 151.8 %all-gather.3.cloned.1.call-start = ((), (), s32[]{:S(2)}) async-start(), calls=%async_computation.3 | async-start | bytes 11943936 | tf_op jit(solution)/shard_map/all_gather | solution.py:686
  8.5 1.7 copy-start.1
  8.5 33.2 %copy-start.13 = (bf16[96]{0:T(256)(128)(2,1)S(1)}, bf16[96]{0:T(256)(128)(2,1)}, u32[]{:S(2)}) copy-start(bf16[96]{0:T(256)(128)(2,1)} %param.12) | copy-start | bytes 580
  8.5 33.1 %copy-start.14 = (bf16[96]{0:T(256)(128)(2,1)S(1)}, bf16[96]{0:T(256)(128)(2,1)}, u32[]{:S(2)}) copy-start(bf16[96]{0:T(256)(128)(2,1)} %param.13) | copy-start | bytes 580
  8.5 33.1 %copy-start.15 = (bf16[96]{0:T(256)(128)(2,1)S(1)}, bf16[96]{0:T(256)(128)(2,1)}, u32[]{:S(2)}) copy-start(bf16[96]{0:T(256)(128)(2,1)} %param.14) | copy-start | bytes 580
  8.5 33.1 %copy-start.16 = (bf16[96]{0:T(256)(128)(2,1)S(1)}, bf16[96]{0:T(256)(128)(2,1)}, u32[]{:S(2)}) copy-start(bf16[96]{0:T(256)(128)(2,1)} %param.17) | copy-start | bytes 580
  8.5 33.1 %copy-start.17 = (bf16[96]{0:T(256)(128)(2,1)S(1)}, bf16[96]{0:T(256)(128)(2,1)}, u32[]{:S(2)}) copy-start(bf16[96]{0:T(256)(128)(2,1)} %param.18) | copy-start | bytes 580
  9.7 354.4 %reduce-scatter.2.cloned.1.call-start = ((), (), s32[]{:S(2)}) async-start(), calls=%async_computation.1 | async-start | bytes 11943936 | tf_op jit(solution)/shard_map/reduce_scatter | solution.py:734
  10.2 29.7 %collective-permute-start = (bf16[768,768]{1,0:T(8,128)(2,1)S(1)}, bf16[768,768]{1,0:T(8,128)(2,1)S(1)}, u32[]{:S(2)}, u32[]{:S(2)}) collective-permute-start(bf16[768,768]{1,0:T(8,128)(2,1)S(1)} %bitcast.68), channel_id=1, source_target_pairs={{0,1},{1,0},{2,4},{3,5},{4,2},{5,3},{6,7},{7,6},{8,9},{9,8},{10,12... | collective-permute-start | bytes 3538952 | tf_op jit(solution)/shard_map/ppermute | solution.py:634
  39.9 8.7 %copy-start = (bf16[768,768]{1,0:T(8,128)(2,1)}, bf16[768,768]{1,0:T(8,128)(2,1)S(1)}, u32[]{:S(2)}) copy-start(bf16[768,768]{1,0:T(8,128)(2,1)S(1)} %collective-permute-done.stay1.move0.tok_m) | copy-start | bytes 3538948
  39.9 9.3 %collective-permute-start.1 = (bf16[768,768]{1,0:T(8,128)(2,1)S(1)}, bf16[768,768]{1,0:T(8,128)(2,1)}, u32[]{:S(2)}, u32[]{:S(2)}) collective-permute-start(bf16[768,768]{1,0:T(8,128)(2,1)S(1)} %collective-permute-done.stay1.move0.tok_m), channel_id=1, source_target_pairs={{2,3},{3,2},{4,5},{5,4},{10,11},{11,10},{12,13},{13,12},{18,19},{1... | collective-permute-start | bytes 3538952 | tf_op jit(solution)/shard_map/ppermute | solution.py:634
  46.7 10.7 %collective-permute-start.5 = (bf16[96,640]{1,0:T(8,128)(2,1)}, bf16[96,640]{1,0:T(8,128)(2,1)}, u32[]{:S(2)}, u32[]{:S(2)}) collective-permute-start(bf16[96,640]{1,0:T(8,128)(2,1)} %get-tuple-element.84), channel_id=1, source_target_pairs={{0,4},{1,5},{2,6},{3,7},{4,0},{5,1},{6,2},{7,3},{8,12},{9,13},{10,... | collective-permute-start | bytes 368648 | tf_op jit(solution)/shard_map/ppermute | solution.py:634
  48.7 46.1 %collective-permute-start.8 = (bf16[768,768]{1,0:T(8,128)(2,1)S(1)}, bf16[768,768]{1,0:T(8,128)(2,1)}, u32[]{:S(2)}, u32[]{:S(2)}) collective-permute-start(bf16[768,768]{1,0:T(8,128)(2,1)S(1)} %bitcast.69), channel_id=1, source_target_pairs={{0,4},{1,5},{2,6},{3,7},{4,0},{5,1},{6,2},{7,3},{8,12},{9,13},{10,... | collective-permute-start | bytes 3538952 | tf_op jit(solution)/shard_map/ppermute | solution.py:634
  48.7 46.1 %collective-permute-start.3 = (bf16[768,768]{1,0:T(8,128)(2,1)S(1)}, bf16[768,768]{1,0:T(8,128)(2,1)S(1)}, u32[]{:S(2)}, u32[]{:S(2)}) collective-permute-start(bf16[768,768]{1,0:T(8,128)(2,1)S(1)} %collective-permute-done.stay1.move0.tok_m), channel_id=1, source_target_pairs={{0,4},{1,5},{2,6},{3,7},{4,0},{5,1},{6,2},{7,3},{8,12},{9,13},{10,... | collective-permute-start | bytes 3538952 | tf_op jit(solution)/shard_map/ppermute | solution.py:634
  49.2 55.1 %collective-permute-start.4 = (bf16[768,768]{1,0:T(8,128)(2,1)}, bf16[768,768]{1,0:T(8,128)(2,1)}, u32[]{:S(2)}, u32[]{:S(2)}) collective-permute-start(bf16[768,768]{1,0:T(8,128)(2,1)} %collective-permute-done.1.move1), channel_id=1, source_target_pairs={{0,4},{1,5},{2,6},{3,7},{4,0},{5,1},{6,2},{7,3},{8,12},{9,13},{10,... | collective-permute-start | bytes 3538952 | tf_op jit(solution)/shard_map/ppermute | solution.py:634
  59.2 14.1 %collective-permute-start.6 = (bf16[2,96,640]{2,1,0:T(8,128)(2,1)}, bf16[2,96,640]{2,1,0:T(8,128)(2,1)}, u32[]{:S(2)}, u32[]{:S(2)}) collective-permute-start(bf16[2,96,640]{2,1,0:T(8,128)(2,1)} %maximum_select_fusion.3), channel_id=1, source_target_pairs={{0,8},{1,9},{2,10},{3,11},{4,12},{5,13},{6,14},{7,15},{8,0},{9,1},... | collective-permute-start | bytes 737288 | tf_op jit(solution)/shard_map/ppermute | solution.py:634
  75.5 12.6 %collective-permute-start.7 = (bf16[4,96,640]{2,1,0:T(8,128)(2,1)}, bf16[4,96,640]{2,1,0:T(8,128)(2,1)}, u32[]{:S(2)}, u32[]{:S(2)}) collective-permute-start(bf16[4,96,640]{2,1,0:T(8,128)(2,1)} %maximum_select_fusion.1), channel_id=1, source_target_pairs={{0,16},{1,17},{2,18},{3,19},{4,20},{5,21},{6,22},{7,23},{8,24},{9,... | collective-permute-start | bytes 1474568 | tf_op jit(solution)/shard_map/ppermute | solution.py:634
  93.0 55.2 %collective-permute-start.2 = (bf16[768,768]{1,0:T(8,128)(2,1)}, bf16[768,768]{1,0:T(8,128)(2,1)}, u32[]{:S(2)}, u32[]{:S(2)}) collective-permute-start(bf16[768,768]{1,0:T(8,128)(2,1)} %bitcast.75), channel_id=1, source_target_pairs={{2,4},{3,5},{4,2},{5,3},{10,12},{11,13},{12,10},{13,11},{18,20},{1... | collective-permute-start | bytes 3538952 | tf_op jit(solution)/shard_map/ppermute | solution.py:634
  141.8 6.9 %collective-permute-start.9 = (bf16[192,768]{1,0:T(8,128)(2,1)}, bf16[192,768]{1,0:T(8,128)(2,1)S(1)}, u32[]{:S(2)}, u32[]{:S(2)}) collective-permute-start(bf16[192,768]{1,0:T(8,128)(2,1)} %get-tuple-element.47.o1), channel_id=1, source_target_pairs={{0,1},{1,0},{2,3},{3,2},{4,5},{5,4},{6,7},{7,6},{8,9},{9,8},{10,11... | collective-permute-start | bytes 884744 | tf_op jit(solution)/shard_map/ppermute | solution.py:634
  143.5 6.1 %collective-permute-start.10 = (bf16[192,768]{1,0:T(8,128)(2,1)}, bf16[192,768]{1,0:T(8,128)(2,1)S(1)}, u32[]{:S(2)}, u32[]{:S(2)}) collective-permute-start(bf16[192,768]{1,0:T(8,128)(2,1)} %get-tuple-element.48.o2), channel_id=1, source_target_pairs={{0,4},{1,5},{2,6},{3,7},{4,0},{5,1},{6,2},{7,3},{8,12},{9,13},{10,... | collective-permute-start | bytes 884744 | tf_op jit(solution)/shard_map/ppermute | solution.py:634
  148.2 10.8 %collective-permute-start.11 = (bf16[192,768]{1,0:T(8,128)(2,1)}, bf16[192,768]{1,0:T(8,128)(2,1)S(1)}, u32[]{:S(2)}, u32[]{:S(2)}) collective-permute-start(bf16[192,768]{1,0:T(8,128)(2,1)} %get-tuple-element.49.o3), channel_id=1, source_target_pairs={{0,5},{1,4},{2,7},{3,6},{4,1},{5,0},{6,3},{7,2},{8,13},{9,12},{10,... | collective-permute-start | bytes 884744 | tf_op jit(solution)/shard_map/ppermute | solution.py:634
  148.7 10.3 %copy-start.9 = (bf16[192,768]{1,0:T(8,128)(2,1)}, bf16[192,768]{1,0:T(8,128)(2,1)S(1)}, u32[]{:S(2)}) copy-start(bf16[192,768]{1,0:T(8,128)(2,1)S(1)} %collective-permute-done.9.m1) | copy-start | bytes 884740
  149.6 9.4 %copy-start.10 = (bf16[192,768]{1,0:T(8,128)(2,1)}, bf16[192,768]{1,0:T(8,128)(2,1)S(1)}, u32[]{:S(2)}) copy-start(bf16[192,768]{1,0:T(8,128)(2,1)S(1)} %collective-permute-done.10.m2) | copy-start | bytes 884740
  208.0 2.8 copy-start.18
  208.1 228.5 %all-reduce.3.cloned.1.call-start = ((), (), s32[]{:S(2)}) async-start(), calls=%async_computation.2 | async-start | bytes 2654208 | tf_op jit(solution)/shard_map/psum | solution.py:735
  209.0 9.0 %collective-permute-start.12 = (bf16[192,768]{1,0:T(8,128)(2,1)S(1)}, bf16[192,768]{1,0:T(8,128)(2,1)S(1)}, u32[]{:S(2)}, u32[]{:S(2)}) collective-permute-start(bf16[192,768]{1,0:T(8,128)(2,1)S(1)} %copy-done.20), channel_id=1, source_target_pairs={{0,5},{1,4},{2,7},{3,6},{4,1},{5,0},{6,3},{7,2},{8,13},{9,12},{10,... | collective-permute-start | bytes 884744 | tf_op jit(solution)/shard_map/ppermute | solution.py:634
  209.1 15.5 %collective-permute-start.14 = (bf16[192,768]{1,0:T(8,128)(2,1)S(1)}, bf16[192,768]{1,0:T(8,128)(2,1)S(1)}, u32[]{:S(2)}, u32[]{:S(2)}) collective-permute-start(bf16[192,768]{1,0:T(8,128)(2,1)S(1)} %copy-done.19), channel_id=1, source_target_pairs={{0,1},{1,0},{2,3},{3,2},{4,5},{5,4},{6,7},{7,6},{8,9},{9,8},{10,11... | collective-permute-start | bytes 884744 | tf_op jit(solution)/shard_map/ppermute | solution.py:634
  210.8 13.8 %collective-permute-start.15 = (bf16[192,768]{1,0:T(8,128)(2,1)S(1)}, bf16[192,768]{1,0:T(8,128)(2,1)S(1)}, u32[]{:S(2)}, u32[]{:S(2)}) collective-permute-start(bf16[192,768]{1,0:T(8,128)(2,1)S(1)} %copy-done.18), channel_id=1, source_target_pairs={{0,4},{1,5},{2,6},{3,7},{4,0},{5,1},{6,2},{7,3},{8,12},{9,13},{10,... | collective-permute-start | bytes 884744 | tf_op jit(solution)/shard_map/ppermute | solution.py:634
  218.0 6.6 %copy-start.21 = (bf16[192,768]{1,0:T(8,128)(2,1)}, bf16[192,768]{1,0:T(8,128)(2,1)S(1)}, u32[]{:S(2)}) copy-start(bf16[192,768]{1,0:T(8,128)(2,1)S(1)} %collective-permute-done.12.g3) | copy-start | bytes 884740
  291.8 3.2 copy-start.5
  291.8 3.2 collective-permute-start.17
  293.3 13.6 %collective-permute-start.25 = (bf16[4,96,576]{2,1,0:T(8,128)(2,1)S(1)}, bf16[4,96,576]{2,1,0:T(8,128)(2,1)S(1)}, u32[]{:S(2)}, u32[]{:S(2)}) collective-permute-start(bf16[4,96,576]{2,1,0:T(8,128)(2,1)S(1)} %bitcast.78), channel_id=1, source_target_pairs={{0,16},{1,17},{2,18},{3,19},{4,20},{5,21},{6,22},{7,23},{8,24},{9,... | collective-permute-start | bytes 1327112 | tf_op jit(solution)/shard_map/ppermute | solution.py:634
  294.9 56.3 %collective-permute-start.16 = (bf16[768,768]{1,0:T(8,128)(2,1)}, bf16[768,768]{1,0:T(8,128)(2,1)S(1)}, u32[]{:S(2)}, u32[]{:S(2)}) collective-permute-start(bf16[768,768]{1,0:T(8,128)(2,1)} %get-tuple-element.59), channel_id=1, source_target_pairs={{0,4},{1,5},{2,6},{3,7},{4,0},{5,1},{6,2},{7,3},{8,12},{9,13},{10,... | collective-permute-start | bytes 3538952 | tf_op jit(solution)/shard_map/ppermute | solution.py:634
  295.3 13.4 %copy-start.6 = (bf16[768,768]{1,0:T(8,128)(2,1)S(1)}, bf16[768,768]{1,0:T(8,128)(2,1)}, u32[]{:S(2)}) copy-start(bf16[768,768]{1,0:T(8,128)(2,1)} %get-tuple-element.52) | copy-start | bytes 3538948
  295.3 55.9 %collective-permute-start.18 = (bf16[768,768]{1,0:T(8,128)(2,1)S(1)}, bf16[768,768]{1,0:T(8,128)(2,1)}, u32[]{:S(2)}, u32[]{:S(2)}) collective-permute-start(bf16[768,768]{1,0:T(8,128)(2,1)S(1)} %add_convert_fusion), channel_id=1, source_target_pairs={{0,1},{1,0},{2,3},{3,2},{4,5},{5,4},{6,7},{7,6},{8,9},{9,8},{10,11... | collective-permute-start | bytes 3538952 | tf_op jit(solution)/shard_map/ppermute | solution.py:634
  307.1 7.7 %collective-permute-start.26 = (bf16[2,96,576]{2,1,0:T(8,128)(2,1)S(1)}, bf16[2,96,576]{2,1,0:T(8,128)(2,1)S(1)}, u32[]{:S(2)}, u32[]{:S(2)}) collective-permute-start(bf16[2,96,576]{2,1,0:T(8,128)(2,1)S(1)} %broadcast_select_fusion.2), channel_id=1, source_target_pairs={{0,8},{1,9},{2,10},{3,11},{4,12},{5,13},{6,14},{7,15},{8,0},{9,1},... | collective-permute-start | bytes 663560 | tf_op jit(solution)/shard_map/ppermute | solution.py:634
  308.7 62.6 %collective-permute-start.13 = (bf16[768,768]{1,0:T(8,128)(2,1)S(1)}, bf16[768,768]{1,0:T(8,128)(2,1)}, u32[]{:S(2)}, u32[]{:S(2)}) collective-permute-start(bf16[768,768]{1,0:T(8,128)(2,1)S(1)} %copy-done.6), channel_id=1, source_target_pairs={{2,4},{3,5},{4,2},{5,3},{10,12},{11,13},{12,10},{13,11},{18,20},{1... | collective-permute-start | bytes 3538952 | tf_op jit(solution)/shard_map/ppermute | solution.py:634
  315.5 34.5 %collective-permute-start.27 = (bf16[2,96,576]{2,1,0:T(8,128)(2,1)}, bf16[2,96,576]{2,1,0:T(8,128)(2,1)}, u32[]{:S(2)}, u32[]{:S(2)}) collective-permute-start(bf16[2,96,576]{2,1,0:T(8,128)(2,1)} %add_convert_fusion.2), channel_id=1, source_target_pairs={{0,2},{1,3},{2,0},{3,1},{4,6},{5,7},{6,4},{7,5},{8,10},{9,11},{10,... | collective-permute-start | bytes 663560 | tf_op jit(solution)/shard_map/ppermute | solution.py:634
  359.8 52.5 %collective-permute-start.19 = (bf16[768,768]{1,0:T(8,128)(2,1)}, bf16[768,768]{1,0:T(8,128)(2,1)S(1)}, u32[]{:S(2)}, u32[]{:S(2)}) collective-permute-start(bf16[768,768]{1,0:T(8,128)(2,1)} %get-tuple-element.65), channel_id=1, source_target_pairs={{2,4},{3,5},{4,2},{5,3},{10,12},{11,13},{12,10},{13,11},{18,20},{1... | collective-permute-start | bytes 3538952 | tf_op jit(solution)/shard_map/ppermute | solution.py:634
  360.6 3.6 collective-permute-start.28
  361.5 1.4 collective-permute-start.20
  363.6 3.8 collective-permute-start.21
  364.2 39.4 %collective-permute-start.29 = (bf16[2,96,576]{2,1,0:T(8,128)(2,1)S(1)}, bf16[2,96,576]{2,1,0:T(8,128)(2,1)S(1)}, u32[]{:S(2)}, u32[]{:S(2)}) collective-permute-start(bf16[2,96,576]{2,1,0:T(8,128)(2,1)S(1)} %maximum_select_fusion.4), channel_id=1, source_target_pairs={{0,1},{1,0},{2,3},{3,2},{4,5},{5,4},{6,7},{7,6},{8,9},{9,8},{10,11... | collective-permute-start | bytes 663560 | tf_op jit(solution)/shard_map/ppermute | solution.py:634
  367.4 3.8 collective-permute-start.22
  371.3 11.0 %collective-permute-start.23 = (f32[8,768]{1,0:T(8,128)S(1)}, f32[8,768]{1,0:T(8,128)S(1)}, u32[]{:S(2)}, u32[]{:S(2)}) collective-permute-start(f32[8,768]{1,0:T(8,128)S(1)} %add.52), channel_id=1, source_target_pairs={{0,1},{1,0},{2,3},{3,2},{4,5},{5,4},{6,7},{7,6},{8,9},{9,8},{10,11... | collective-permute-start | bytes 73736 | tf_op jit(solution)/shard_map/ppermute | solution.py:634
  382.9 28.1 %collective-permute-start.24 = (f32[8,768]{1,0:T(8,128)}, f32[8,768]{1,0:T(8,128)}, u32[]{:S(2)}, u32[]{:S(2)}) collective-permute-start(f32[8,768]{1,0:T(8,128)} %add.53), channel_id=1, source_target_pairs={{0,2},{1,3},{2,0},{3,1},{4,6},{5,7},{6,4},{7,5},{8,10},{9,11},{10,... | collective-permute-start | bytes 73736 | tf_op jit(solution)/shard_map/ppermute | solution.py:634
  438.6 1.7 copy-start.2
  (9 other events, 8.6 us)
Sparse Core Ops, SparseCore 0:
  10.5 71.3 all-gather.2
  208.2 82.1 reduce-scatter.1
  364.3 72.2 all-reduce.2
